TPU v7x, 256 devices: a whole 4x4x8 slice. The times are simulated.
256 devices in a mesh: gen: 32 (over z, y_lo, core), neur: 4 (over x), box: 2 (over y_hi).
Axes of the slice: x: 4, y: 4 (y_hi: 2, y_lo: 2; y = y_hi * 2 + y_lo), z: 8, core: 2. Of those that a mesh axis runs over, the one named last changes fastest.
Arguments:
- gens: bfloat16 [8, 1024, 4096], P('box', 'gen'), may hold values from -1 to 1
- center: bfloat16 [8, 4096], P('box'), may hold values from -6 to 6
- weight: bfloat16 [4096, 2048], P('gen', 'neur'), may hold values from -0.09375 to 0.09375
- bias: float32 [2048], P('neur'), may hold values from -3 to 3
- phase: int32 [8, 2048], P('box', 'neur'), may hold values from 0 to 2
- gens_cot: bfloat16 [8, 1024, 2048], P('box', 'gen', 'neur'), may hold values from -6 to 6
- center_cot: float32 [8, 2048], P('box', 'neur'), may hold values from -6 to 6
- offset_cot: float32 [8, 2048], P('box', 'neur'), may hold values from -6 to 6
Outputs:
- center_out: float32 [8, 2048], P('box', 'neur')
- gens_out: bfloat16 [8, 1024, 2048], P('box', 'gen', 'neur')
- offset: float32 [8, 2048], P('box', 'neur')
- weight_grad: float32 [4096, 2048], P('gen', 'neur')
- bias_grad: float32 [2048], P('neur')
- gens_grad: float32 [8, 1024, 4096], P('box', 'gen', 'neur')
- center_grad: float32 [8, 4096], P('box', 'neur')
Inputs may be any that keep to these rules, and one draw needn't show every extreme that they name: `phase`: 0 marks an inactive neuron, 1 an active one, 2 one that crosses zero.
All inputs are finite; a program needn't handle non-finite values.
Results may differ from a plain program's by a relative error of at most 0.006.
Values may be sent and summed in bfloat16 or wider, within the bound.
A program may use at most 64 MiB of HBM per device.

v0:
```python
import jax
import jax.numpy as jnp
from jax import lax
from jax.sharding import PartitionSpec as P


def neuron(center_pre, radius, phase):
    upper = center_pre + radius
    lower = center_pre - radius
    ratio = jnp.clip(upper / (upper - lower + 1e-05), 0.0, 1.0)
    active = (phase == 1).astype(center_pre.dtype)
    crossing = (phase == 2).astype(center_pre.dtype)
    slope = active + crossing * ratio
    offset = crossing * (-ratio * lower * 0.5)
    return (slope, slope * center_pre + offset, offset)


def body(gens, center, weight, bias, phase, gens_cot, center_cot, offset_cot):
    box_dev, gen_dev, width = gens.shape
    local_cols = weight.shape[1]
    local_rows = box_dev * gen_dev
    wide = jnp.concatenate([gens.reshape(local_rows, width), center], 0)
    full_weight = lax.all_gather(weight, "gen", axis=0, tiled=True)
    product = jnp.dot(wide, full_weight, preferred_element_type=jnp.float32)
    gen_pre = product[:local_rows].reshape(box_dev, gen_dev, local_cols)
    center_pre = product[local_rows:] + bias
    part_radius = jnp.sum(jnp.abs(gen_pre), axis=1)
    cot_wide = gens_cot.astype(jnp.float32)
    radius = lax.psum(part_radius, "gen")
    slope, center_out, offset = neuron(center_pre, radius, phase)
    gens_out = (slope[:, None, :] * gen_pre).astype(jnp.bfloat16)
    intersection = lax.psum(jnp.sum(cot_wide * gen_pre, axis=1), "gen")
    unused, pull = jax.vjp(lambda a, b: neuron(a, b, phase), center_pre, radius)
    g_center, g_radius = pull((intersection, center_cot, offset_cot))
    gen_back = (slope[:, None, :] * cot_wide + jnp.sign(gen_pre) * g_radius[:, None, :]).astype(
        jnp.bfloat16
    )
    center_back = g_center.astype(jnp.bfloat16)
    back = jnp.concatenate([gen_back.reshape(local_rows, local_cols), center_back], 0)
    first_gen = (lax.axis_index("gen") == 0).astype(jnp.bfloat16)
    back_owned = jnp.concatenate(
        [gen_back.reshape(local_rows, local_cols), center_back * first_gen], 0
    )
    bias_part = jnp.sum(g_center, axis=0)
    shares = lax.psum_scatter(
        lax.dot_general(
            wide, back_owned, (((0,), (0,)), ((), ())), preferred_element_type=jnp.float32
        ),
        "gen",
        scatter_dimension=0,
        tiled=True,
    )
    weight_grad, bias_grad = lax.psum((shares, bias_part), "box")
    partial_back = lax.dot_general(
        back, full_weight, (((1,), (1,)), ((), ())), preferred_element_type=jnp.float32
    )
    summed = lax.psum_scatter(partial_back, "neur", scatter_dimension=1, tiled=True)
    gens_grad = summed[:local_rows].reshape(box_dev, gen_dev, summed.shape[1])
    center_grad = summed[local_rows:]
    return (center_out, gens_out, offset, weight_grad, bias_grad, gens_grad, center_grad)


def solution(mesh):
    return jax.shard_map(
        body,
        mesh=mesh,
        in_specs=(
            P("box", "gen", None),
            P("box", None),
            P("gen", "neur"),
            P("neur"),
            P("box", "neur"),
            P("box", "gen", "neur"),
            P("box", "neur"),
            P("box", "neur"),
        ),
        out_specs=(
            P("box", "neur"),
            P("box", "gen", "neur"),
            P("box", "neur"),
            P("gen", "neur"),
            P("neur"),
            P("box", "gen", "neur"),
            P("box", "neur"),
        ),
        check_vma=False,
    )
```

profile of v0, /device:TPU:1, one launch (start us, length us, event | category | flops | bytes accessed | tf_op | source)
XLA Modules:
  0.0 407.0 jit_solution(1934625204832896701)
XLA Ops:
  7.2 0.0 all-gather.2.cloned.1.call-start
  7.2 0.7 all-gather.2.cloned.1.call-update
  7.9 0.0 reduce-scatter.3.cloned.1.call-start
  8.0 72.6 %all-gather.2.cloned.1.call-done = bf16[4096,512]{1,0:T(8,128)(2,1)} async-done(((bf16[128,512]{1,0:T(8,128)(2,1)}), bf16[4096,512]{1,0:T(8,128)(2,1)}) %all-gather.2.cloned.1.call-update) | async-done | bytes 4194320 | tf_op jit(solution)/shard_map/all_gather | solution.py:23
  80.6 0.0 copy-start.1
  80.6 0.0 copy-start.3
  80.6 0.0 copy-start.4
  80.6 0.0 copy-start.5
  80.6 0.0 copy-start.6
  80.6 0.0 copy-start
  80.6 0.0 copy-start.2
  80.6 3.4 fusion.1
  84.0 0.0 copy-done.1
  84.0 0.1 fusion.4
  84.1 101.8 %all-reduce = (f32[4,512]{1,0:T(4,128)S(1)}, f32[4,512]{1,0:T(4,128)S(1)}) all-reduce(f32[4,512]{1,0:T(4,128)S(1)} %get-tuple-element.8, f32[4,512]{1,0:T(4,128)S(1)} %get-tuple-element.7), channel_id=1, replica_groups=mesh['gen'=32,'neur'=4,'box'=2] {'gen'}, use_global_device_ids=true, to_apply=%region_1.0 | all-reduce | flops 4096 | bytes 32768 | tf_op jit(solution)/shard_map/psum | solution.py:29
  185.9 0.0 copy-done.3
  185.9 0.0 copy-done.4
  185.9 0.0 copy-done.5
  185.9 0.0 copy-done.6
  186.0 0.8 fusion.3
  186.8 0.0 copy-done
  186.8 0.0 copy-done.2
  186.8 4.6 %fusion = f32[4096,512]{1,0:T(8,128)} fusion(bf16[4,4096]{1,0:T(4,128)(2,1)S(1)} %copy-done.2, bf16[128,4096]{1,0:T(8,128)(2,1)S(1)} %bitcast.13, bf16[4,512]{1,0:T(4,128)(2,1)S(1)} %get-tuple-element.16, bf16[128,512]{1,0:T(8,128)(2,1)S(1)} %bitcast.10), kind=kOutput, calls=%fused_computation.1 | convolution fusion | flops 556081152 | bytes 9605120 | tf_op jit(solution)/shard_map/dot_general | solution.py:46
  191.3 0.0 reduce-scatter.3.cloned.1.call-update
  191.4 0.0 reduce-scatter.5.cloned.1.call-start
  191.4 5.1 %fusion.7 = f32[132,4096]{1,0:T(8,128)} fusion(bf16[4096,512]{1,0:T(8,128)(2,1)} %all-gather.2.cloned.1.call-done, bf16[4,512]{1,0:T(4,128)(2,1)S(1)} %get-tuple-element.17, bf16[128,512]{1,0:T(8,128)(2,1)S(1)} %bitcast.11), kind=kOutput, calls=%fused_computation.12 | convolution fusion | flops 553918464 | bytes 6492160 | tf_op jit(solution)/shard_map/dot_general | solution.py:54
  196.5 0.0 reduce-scatter.5.cloned.1.call-update
  196.5 0.0 all-reduce.3.cloned.1.call-start
  196.5 126.5 %reduce-scatter.3.cloned.1.call-done = f32[128,512]{1,0:T(8,128)} async-done(((f32[4096,512]{1,0:T(8,128)}), f32[128,512]{1,0:T(8,128)}) %reduce-scatter.3.cloned.1.call-update) | async-done | bytes 262160 | tf_op jit(solution)/shard_map/reduce_scatter | solution.py:45
  323.1 0.0 all-reduce.3.cloned.1.call-update
  323.1 5.9 %psum.31 = f32[512]{0:T(512)} all-reduce(f32[512]{0:T(512)S(1)} %get-tuple-element.11), channel_id=1, replica_groups=mesh['gen'=32,'neur'=4,'box'=2] {'box'}, use_global_device_ids=true, to_apply=%region_7.8 | all-reduce | flops 512 | bytes 4096 | tf_op jit(solution)/shard_map/psum | solution.py:53
  328.9 0.6 multiply_add_fusion.1
  329.6 30.9 %reduce-scatter.5.cloned.1.call-done = f32[132,1024]{1,0:T(8,128)} async-done(((f32[132,4096]{1,0:T(8,128)}), f32[132,1024]{1,0:T(8,128)}) %reduce-scatter.5.cloned.1.call-update) | async-done | bytes 540688 | tf_op jit(solution)/shard_map/reduce_scatter | solution.py:57
  360.5 1.4 slice.19
  361.9 1.9 slice.18
  363.7 35.1 %all-reduce.3.cloned.1.call-done = f32[128,512]{1,0:T(8,128)} async-done(((f32[128,512]{1,0:T(8,128)}), f32[128,512]{1,0:T(8,128)}) %all-reduce.3.cloned.1.call-update) | async-done | bytes 262160 | tf_op jit(solution)/shard_map/psum | solution.py:53
  398.8 1.7 copy.16
  (4 shorter events, 0.1 us)
Async XLA Ops:
  7.2 73.4 %all-gather.2.cloned.1.call-start = ((), (), s32[]{:S(2)}) async-start(), calls=%async_computation.2 | async-start | bytes 4325376 | tf_op jit(solution)/shard_map/all_gather | solution.py:23
  7.9 315.1 %reduce-scatter.3.cloned.1.call-start = ((), (), s32[]{:S(2)}) async-start(), calls=%async_computation.3 | async-start | bytes 8650752 | tf_op jit(solution)/shard_map/reduce_scatter | solution.py:45
  80.6 3.4 copy-start.1
  80.6 105.3 %copy-start.3 = (f32[4,512]{1,0:T(4,128)S(1)}, f32[4,512]{1,0:T(4,128)}, u32[]{:S(2)}) copy-start(f32[4,512]{1,0:T(4,128)} %param.14) | copy-start | bytes 24580
  80.6 105.3 %copy-start.4 = (f32[4,512]{1,0:T(4,128)S(1)}, f32[4,512]{1,0:T(4,128)}, u32[]{:S(2)}) copy-start(f32[4,512]{1,0:T(4,128)} %param.15) | copy-start | bytes 24580
  80.6 105.3 %copy-start.5 = (s32[4,512]{1,0:T(4,128)S(1)}, s32[4,512]{1,0:T(4,128)}, u32[]{:S(2)}) copy-start(s32[4,512]{1,0:T(4,128)} %param.12) | copy-start | bytes 24580
  80.6 105.3 %copy-start.6 = (f32[512]{0:T(512)S(1)}, f32[512]{0:T(512)}, u32[]{:S(2)}) copy-start(f32[512]{0:T(512)} %param.11) | copy-start | bytes 6148
  80.6 106.2 %copy-start = (bf16[4,32,4096]{2,1,0:T(8,128)(2,1)S(1)}, bf16[4,32,4096]{2,1,0:T(8,128)(2,1)}, u32[]{:S(2)}) copy-start(bf16[4,32,4096]{2,1,0:T(8,128)(2,1)} %param.8) | copy-start | bytes 3145732
  80.6 106.2 %copy-start.2 = (bf16[4,4096]{1,0:T(4,128)(2,1)S(1)}, bf16[4,4096]{1,0:T(4,128)(2,1)}, u32[]{:S(2)}) copy-start(bf16[4,4096]{1,0:T(4,128)(2,1)} %param.9) | copy-start | bytes 98308
  191.4 169.1 %reduce-scatter.5.cloned.1.call-start = ((), (), s32[]{:S(2)}) async-start(), calls=%async_computation.5 | async-start | bytes 2785280 | tf_op jit(solution)/shard_map/reduce_scatter | solution.py:57
  196.5 202.3 %all-reduce.3.cloned.1.call-start = ((), (), s32[]{:S(2)}) async-start(), calls=%async_computation.4 | async-start | bytes 524288 | tf_op jit(solution)/shard_map/psum | solution.py:53
Sparse Core Ops, SparseCore 0:
  9.8 70.6 all-gather.1
  191.5 131.5 reduce-scatter.2
  325.6 34.8 reduce-scatter.4
  362.9 35.8 all-reduce.2
where the time goes:
time: 407 us
  waiting for transfers between devices  266 us (65%)
  blocking collectives  108 us (27%)
  between operations  13.9 us (3%)
  matrix products  13 us (3%)
  local copies, waits for them, and re-layouts  4.95 us (1%)
    reduce_scatter x1, waiting for transfers between devices, body(): lax.psum_scatter(lax.dot_general(wide, back_owned, (((0,), (0,)), ((), ()...  127 us
    psum x1, blocking collectives, body(): radius = lax.psum(part_radius, 'gen')  102 us
    all_gather x1, waiting for transfers between devices, body(): full_weight = lax.all_gather(weight, 'gen', axis=0, tiled=True)  72.6 us
    psum x1, waiting for transfers between devices, body(): weight_grad, bias_grad = lax.psum((shares, bias_part), 'box')  35.1 us
    reduce_scatter x1, waiting for transfers between devices, body(): lax.psum_scatter(partial_back, 'neur', scatter_dimension=1, tiled=True)  30.9 us
  transfers between devices with their start and end apart: 4, of which 4 were waited for; matrix products, arithmetic and copies ran while one was open for 2% of the time, Pallas kernels for 0%

commit v1 on v0

v1 whole, which is shorter than its diff:
```python
import functools

import jax
import jax.numpy as jnp
from jax import lax
from jax.experimental import pallas as pl
from jax.experimental.pallas import tpu as pltpu
from jax.sharding import PartitionSpec as P

MESH = pl.DeviceIdType.MESH
F32 = jnp.float32
BF16 = jnp.bfloat16

NZ = 8
D = 4096
COLS = 512
ROWS = 128
WIDE = 144


def neuron(center_pre, radius, phase):
    upper = center_pre + radius
    lower = center_pre - radius
    ratio = jnp.clip(upper / (upper - lower + 1e-05), 0.0, 1.0)
    active = (phase == 1).astype(center_pre.dtype)
    crossing = (phase == 2).astype(center_pre.dtype)
    slope = active + crossing * ratio
    offset = crossing * (-ratio * lower * 0.5)
    return (slope, slope * center_pre + offset, offset)


def copy_to(src, dst, send_sem, recv_sem, device):
    return pltpu.make_async_remote_copy(
        src_ref=src,
        dst_ref=dst,
        send_sem=send_sem,
        recv_sem=recv_sem,
        device_id=device,
        device_id_type=MESH,
    )


def zsteps(d):
    return {0: (0,), 4: (4,)}.get(d, (-d, d))


def kernel(
    gens_hbm, center_ref, w_hbm, bias_ref, phase_ref, cot_ref, ccot_ref, ocot_ref,
    cout_ref, gout_ref, off_ref, wg_ref, bg_ref, gg_ref, cg_ref,
    w, wide, acc, cslot, gt, amat, sa, sb, bk, bmat, cmat, zs, zr, gs, gr, fx, xb,
    load_sem, w_send, w_recv, a_send, a_recv, ax_send, ax_recv,
    sa_send, sa_recv, sb_send, sb_recv, b_send, b_recv, bp_send,
    g_send, g_recv, z_send, z_recv, f_send, f_recv, x_send, x_recv,
):
    me = lax.axis_index("gen")
    x = lax.axis_index("neur")
    yhi = lax.axis_index("box")
    z = me // 4
    ylo = (me // 2) % 2
    c = me % 2
    y = yhi * 2 + ylo
    quad = ylo * 2 + c

    def dev(zz, yy, cc, xx=None):
        return (zz * 4 + (yy % 2) * 2 + cc, x if xx is None else xx, yy // 2)

    def zdev(k):
        return dev((z + NZ + k) % NZ, y, c)

    def ydev(k, cc=None):
        return dev(z, (y + k) % 4, c if cc is None else cc)

    def xdev(k):
        return dev(z, y, c, (x + k) % 4)

    partner = dev(z, y, 1 - c)
    other_box = ydev(2)

    load_w = pltpu.make_async_copy(w_hbm, w.at[pl.ds(pl.multiple_of(me * 128, 128), 128)], load_sem.at[0])
    load_g = pltpu.make_async_copy(gens_hbm, wide.at[pl.ds(0, ROWS)], load_sem.at[1])
    load_w.start()
    load_g.start()

    barrier = pltpu.get_barrier_semaphore()
    peers = [partner] + [zdev(k) for k in range(1, NZ)] + [xdev(k) for k in (1, 2, 3)]
    peers += [ydev(k, cc) for k in (1, 2, 3) for cc in (0, 1)]
    for peer in peers:
        pl.semaphore_signal(barrier, inc=1, device_id=peer, device_id_type=MESH)

    wide[pl.ds(ROWS, 16)] = jnp.concatenate([center_ref[...].astype(F32), jnp.zeros((12, D), F32)], 0).astype(BF16)
    acc[...] = jnp.zeros_like(acc)
    bk[pl.ds(ROWS, 16)] = jnp.zeros((16, COLS), BF16)
    load_w.wait()
    load_g.wait()
    pl.semaphore_wait(barrier, len(peers))

    def half(zz, yl, cc, h):
        g = zz * 4 + yl * 2 + cc
        return w.at[pl.ds(pl.multiple_of(g * 128 + h * 64, 64), 64)], g * 2 + h

    def wcopy(kind, zz, yl, cc, h):
        ref, at = half(zz, yl, cc, h)
        if kind == 2:
            to = ydev(1) if h == 0 else ydev(3)
        else:
            to = (zdev(1), zdev(-1), None, partner)[kind]
        return copy_to(ref, ref, w_send.at[kind, at], w_recv.at[at], to)

    sent = []

    def send(kind, zz, yl, cc, h):
        cp = wcopy(kind, zz, yl, cc, h)
        cp.start()
        sent.append(cp)

    def arrived(zz, yl, cc, h):
        wcopy(3, zz, yl, cc, h).wait_recv()

    for h in (0, 1):
        send(0, z, ylo, c, h)
        send(1, z, ylo, c, 1 - h)
    for h in (0, 1):
        send(2, z, ylo, c, h)
    for h in (0, 1):
        send(3, z, ylo, c, h)

    def turn(i, carry):
        at = pl.multiple_of(i * 128, 128)
        gt[pl.ds(at, 128), :] = wide[0:ROWS, pl.ds(at, 128)].astype(F32).T.astype(BF16)
        return carry

    lax.fori_loop(0, D // 128, turn, 0)
    gt3 = gt.reshape(NZ, 512, 128)

    def a_rows(yy, cc):
        return pl.ds(pl.multiple_of((yy % 2) * 256 + cc * 128 + (yy // 2) * 64, 64), 64)

    def lanes(at, n=128):
        return pl.ds(pl.multiple_of(at, 128), n)

    mine = pl.ds(2 * x, 2)
    a_sent = []
    for k in (1, 3, 2):
        r = 4 - k
        for cc in (0, 1):
            cp = copy_to(
                gt3.at[mine, a_rows((y + k) % 4, cc), :],
                amat.at[mine, :, lanes((r * 2 + c) * 128)],
                a_send.at[k * 2 + cc],
                a_recv.at[r * 2 + c],
                ydev(k, cc),
            )
            cp.start()
            a_sent.append(cp)
    cp = copy_to(gt3.at[:, a_rows(y, 1 - c), :], amat.at[:, :, lanes(c * 128)], a_send.at[0], a_recv.at[c], partner)
    cp.start()
    a_sent.append(cp)
    own_a = pltpu.make_async_copy(gt3.at[:, a_rows(y, c), :], amat.at[:, :, lanes(c * 128)], load_sem.at[2])
    own_a.start()

    def a_spread():
        for r in (1, 2, 3):
            for cc in (0, 1):
                ref = amat.at[mine, :, lanes((r * 2 + cc) * 128)]
                copy_to(ref, ref, a_send.at[1], a_recv.at[r * 2 + cc], partner).wait_recv()
        ref = amat.at[mine, :, lanes(256, 768)]
        for k in (2, 1, 3):
            cp = copy_to(ref, ref, ax_send.at[k - 1], ax_recv.at[3 - k], xdev(k))
            cp.start()
            a_sent.append(cp)

    def handle_y(d):
        for dz in zsteps(d):
            zz = (z + NZ + dz) % NZ
            for h in (0, 1):
                arrived(zz, 1 - ylo, c, h)
                send(3, zz, 1 - ylo, c, h)

    def compute(d):
        for dz in zsteps(d):
            zz = (z + NZ + dz) % NZ
            for yl in (0, 1):
                for h in (0, 1):
                    arrived(zz, yl, 1 - c, h)
            at = pl.ds(pl.multiple_of(zz * 512, 512), 512)
            res = jnp.dot(wide[:, at], w[at, :], preferred_element_type=F32)
            acc[...] += res[:ROWS]
            cslot[zz] = res[ROWS : ROWS + 8]

    for d in (1, 2, 3, 4):
        for h in (0, 1):
            for way in (0, 1):
                hh = h if way == 0 else 1 - h
                if d == 4 and hh != way:
                    continue
                zz = (z + NZ - d) % NZ if way == 0 else (z + d) % NZ
                arrived(zz, ylo, c, hh)
                if d < 3 or (d == 3 and hh == way):
                    send(way, zz, ylo, c, hh)
                send(2, zz, ylo, c, hh)
                send(3, zz, ylo, c, hh)
        handle_y(d - 1)
        if d == 2:
            a_spread()
        if d >= 2:
            compute(d - 2)
    handle_y(4)
    compute(3)
    compute(4)

    gen_pre = acc[...]
    cot = cot_ref[...].astype(F32)
    part_radius = jnp.sum(jnp.abs(gen_pre).reshape(4, 32, COLS), axis=1)
    part_inner = jnp.sum((cot * gen_pre).reshape(4, 32, COLS), axis=1)
    sa[quad] = jnp.concatenate([part_radius, part_inner], 0)
    for k in (1, 2, 3):
        q = (quad + k) % 4
        cp = copy_to(sa.at[quad], sa.at[quad], sa_send.at[k], sa_recv.at[quad], (z * 4 + q, x, yhi))
        cp.start()
        sent.append(cp)
    for k in (1, 2, 3):
        q = (quad + k) % 4
        copy_to(sa.at[q], sa.at[q], sa_send.at[0], sa_recv.at[q], partner).wait_recv()
    sb[z] = (sa[0] + sa[1]) + (sa[2] + sa[3])
    for k in (4, 3, 5, 2, 6, 1, 7):
        cp = copy_to(sb.at[z], sb.at[z], sb_send.at[k], sb_recv.at[z], zdev(k))
        cp.start()
        sent.append(cp)
    center_pre = cslot[0][0:4]
    for i in range(1, NZ):
        center_pre = center_pre + cslot[i][0:4]
    center_pre = center_pre + bias_ref[...]
    for k in (1, 7, 2, 6, 3, 5, 4):
        zz = (z + k) % NZ
        copy_to(sb.at[zz], sb.at[zz], sb_send.at[0], sb_recv.at[zz], partner).wait_recv()
    total = ((sb[0] + sb[1]) + (sb[2] + sb[3])) + ((sb[4] + sb[5]) + (sb[6] + sb[7]))
    radius = total[0:4]
    intersection = total[4:8]

    phase = phase_ref[...]
    (slope, center_out, offset), pull = jax.vjp(lambda a, b: neuron(a, b, phase), center_pre, radius)
    g_center, g_radius = pull((intersection, ccot_ref[...], ocot_ref[...]))
    pre3 = gen_pre.reshape(4, 32, COLS)
    sign = jnp.where(pre3 > 0, 1.0, jnp.where(pre3 < 0, -1.0, 0.0))
    back = (slope[:, None, :] * cot.reshape(4, 32, COLS) + sign * g_radius[:, None, :]).astype(BF16).reshape(ROWS, COLS)
    bk[0:ROWS] = back
    own_b = pl.multiple_of(c * 128, 128)
    bmat[pl.ds(own_b, 128)] = back

    def b_ref(r, cc, h):
        return bmat.at[pl.ds(pl.multiple_of((r * 2 + cc) * 128 + h * 64, 64), 64)]

    def b_copy(src, r, cc, h, ssem, to):
        return copy_to(src, b_ref(r, cc, h), ssem, b_recv.at[(r * 2 + cc) * 2 + h], to)

    b_sent = []

    def b_start(cp):
        cp.start()
        b_sent.append(cp)

    for i in (0, 1):
        b_start(b_copy(bk.at[i * 64 : i * 64 + 64], 3, c, i, b_send.at[0, i], ydev(1)))
        j = 1 - i
        b_start(b_copy(bk.at[j * 64 : j * 64 + 64], 1, c, j, b_send.at[1, j], ydev(3)))
    for i in (0, 1):
        b_start(b_copy(bk.at[i * 64 : i * 64 + 64], 0, c, i, b_send.at[2, i], partner))

    center_back = g_center.astype(BF16).astype(F32)
    bk[pl.ds(ROWS, 16)] = jnp.concatenate([center_back, jnp.zeros((12, COLS), F32)], 0).astype(BF16)
    xb[yhi, :, 0:COLS] = jnp.concatenate([center_back, jnp.sum(g_center, axis=0, keepdims=True), jnp.zeros((3, COLS), F32)], 0)
    xb[yhi, :, COLS : COLS + 128] = jnp.concatenate(
        [center_ref[:, lanes(me * 128)].astype(F32), jnp.zeros((4, 128), F32)], 0
    )
    xcp = copy_to(xb.at[yhi], xb.at[yhi], x_send, x_recv, other_box)
    xcp.start()
    cout_ref[...] = center_out
    off_ref[...] = offset
    gout_ref[...] = (slope[:, None, :] * pre3).astype(BF16).reshape(ROWS, COLS)

    def partial(k):
        at = pl.ds(pl.multiple_of(((x + k) % 4) * 1024, 1024), 1024)
        return lax.dot_general(bk[...], w[at, :], (((1,), (1,)), ((), ())), preferred_element_type=F32)

    g_sent = []

    def g_start(k):
        gs[k - 1] = partial(k).astype(BF16)
        cp = copy_to(gs.at[k - 1], gr.at[3 - k], g_send.at[k - 1], g_recv.at[3 - k], xdev(k))
        cp.start()
        g_sent.append(cp)

    def b_arrived(r, cc, h):
        b_copy(b_ref(r, cc, h), r, cc, h, b_send.at[0, 0], partner).wait_recv()

    own_a.wait()
    for r in (1, 2, 3):
        ref = amat.at[mine, :, lanes(256, 768)]
        copy_to(ref, ref, ax_send.at[0], ax_recv.at[r - 1], partner).wait_recv()
    ref = amat.at[:, :, lanes((1 - c) * 128)]
    copy_to(ref, ref, a_send.at[1], a_recv.at[1 - c], partner).wait_recv()

    def c_pass(r, first=False):
        a = amat[:, :, r * 256 : r * 256 + 256].reshape(512, 256)
        res = jnp.dot(a, bmat[r * 256 : r * 256 + 256], preferred_element_type=F32)
        if first:
            cmat[...] = res.reshape(NZ, 64, COLS)
        else:
            cmat[...] += res.reshape(NZ, 64, COLS)

    g_start(2)
    for i in (0, 1):
        for r, h, to in ((3, i, 1), (1, 1 - i, 3)):
            b_arrived(r, c, h)
            if i == 0:
                b_start(b_copy(b_ref(r, c, h), 2, c, h, b_send.at[3, h], ydev(to)))
            b_start(b_copy(b_ref(r, c, h), r, c, h, b_send.at[4 if r == 3 else 5, h], partner))
    for h in (0, 1):
        b_arrived(0, 1 - c, h)
    c_pass(0, True)
    for h in (0, 1):
        b_arrived(2, c, h)
        b_start(b_copy(b_ref(2, c, h), 2, c, h, bp_send.at[h], partner))
    for r in (3, 1):
        for h in (0, 1):
            b_arrived(r, 1 - c, h)
        c_pass(r)
    for h in (0, 1):
        b_arrived(2, 1 - c, h)
    c_pass(2)

    z_sent = []
    for dist in (4, 3, 2, 1, 0):
        for p in (0, 1):
            for way in (0, 1):
                longest = 4 if p == way else 3
                if dist > longest:
                    continue
                zz = (z + NZ + (dist if way == 0 else -dist)) % NZ
                val = cmat[zz, :, p * 256 : p * 256 + 256]
                if dist < longest:
                    cp = copy_to(
                        zr.at[way, dist, p], zr.at[way, dist, p], z_send.at[way, dist, p], z_recv.at[way, dist, p], partner
                    )
                    cp.wait_recv()
                    val = val + zr[way, dist, p].astype(F32)
                if dist > 0:
                    zs[way, dist, p] = val.astype(BF16)
                    cp = copy_to(
                        zs.at[way, dist, p],
                        zr.at[way, dist - 1, p],
                        z_send.at[way, dist, p],
                        z_recv.at[way, dist - 1, p],
                        zdev(1 if way == 0 else -1),
                    )
                    cp.start()
                    z_sent.append(cp)
                elif way == 1:
                    total_p = val + zr[0, 0, p].astype(F32)
                    fx[yhi, :, p * 256 : p * 256 + 256] = total_p.astype(BF16)
        if dist in (4, 3):
            g_start(1 if dist == 4 else 3)
        if dist == 2:
            own = partial(0)
    fcp = copy_to(fx.at[yhi], fx.at[yhi], f_send, f_recv, other_box)
    fcp.start()

    for k in (1, 2, 3):
        copy_to(gr.at[k - 1], gr.at[k - 1], g_send.at[0], g_recv.at[k - 1], partner).wait_recv()
    summed = own + gr[0].astype(F32) + gr[1].astype(F32) + gr[2].astype(F32)
    gg_ref[...] = summed[:ROWS]
    cg_ref[...] = summed[ROWS : ROWS + 4]

    other = 1 - yhi
    copy_to(xb.at[other], xb.at[other], x_send, x_recv, other_box).wait_recv()
    xall = xb[...].reshape(16, COLS + 128)
    term = lax.dot_general(
        xall[:, COLS:].T.astype(BF16), xall[:, :COLS].astype(BF16), (((1,), (0,)), ((), ())), preferred_element_type=F32
    )
    bg_ref[...] = xall[4:5, :COLS] + xall[12:13, :COLS]
    copy_to(fx.at[other], fx.at[other], f_send, f_recv, other_box).wait_recv()
    wg_ref[...] = fx[...].astype(F32).reshape(128, COLS) + term

    for cp in sent + a_sent + b_sent + g_sent + z_sent + [xcp, fcp]:
        cp.wait_send()


def body(gens, center, weight, bias, phase, gens_cot, center_cot, offset_cot):
    vm = pl.BlockSpec(memory_space=pltpu.VMEM)
    hbm = pl.BlockSpec(memory_space=pl.ANY)
    dma = pltpu.SemaphoreType.DMA
    sds = jax.ShapeDtypeStruct
    outs = pl.pallas_call(
        kernel,
        out_shape=(
            sds((4, COLS), F32),
            sds((ROWS, COLS), BF16),
            sds((4, COLS), F32),
            sds((128, COLS), F32),
            sds((1, COLS), F32),
            sds((ROWS, 1024), F32),
            sds((4, 1024), F32),
        ),
        in_specs=[hbm, vm, hbm, vm, vm, vm, vm, vm],
        out_specs=(vm,) * 7,
        scratch_shapes=[
            pltpu.VMEM((D, COLS), BF16),
            pltpu.VMEM((WIDE, D), BF16),
            pltpu.VMEM((ROWS, COLS), F32),
            pltpu.VMEM((NZ, 8, COLS), F32),
            pltpu.VMEM((D, ROWS), BF16),
            pltpu.VMEM((NZ, 64, 1024), BF16),
            pltpu.VMEM((4, 8, COLS), F32),
            pltpu.VMEM((NZ, 8, COLS), F32),
            pltpu.VMEM((WIDE, COLS), BF16),
            pltpu.VMEM((1024, COLS), BF16),
            pltpu.VMEM((NZ, 64, COLS), F32),
            pltpu.VMEM((2, 5, 2, 64, 256), BF16),
            pltpu.VMEM((2, 5, 2, 64, 256), BF16),
            pltpu.VMEM((3, WIDE, 1024), BF16),
            pltpu.VMEM((3, WIDE, 1024), BF16),
            pltpu.VMEM((2, 64, COLS), BF16),
            pltpu.VMEM((2, 8, COLS + 128), F32),
            dma((3,)),
            dma((4, 64)),
            dma((64,)),
            dma((8,)),
            dma((8,)),
            dma((3,)),
            dma((3,)),
            dma((4,)),
            dma((4,)),
            dma((8,)),
            dma((8,)),
            dma((6, 2)),
            dma((16,)),
            dma((2,)),
            dma((3,)),
            dma((3,)),
            dma((2, 5, 2)),
            dma((2, 5, 2)),
            dma,
            dma,
            dma,
            dma,
        ],
        compiler_params=pltpu.CompilerParams(
            collective_id=0, has_side_effects=True, vmem_limit_bytes=56 * 1024 * 1024
        ),
        name="zonotope_step",
    )(
        gens.reshape(ROWS, D), center, weight, bias.reshape(1, COLS), phase,
        gens_cot.reshape(ROWS, COLS), center_cot, offset_cot,
    )
    center_out, gens_out, offset, weight_grad, bias_grad, gens_grad, center_grad = outs
    return (
        center_out, gens_out.reshape(4, 32, COLS), offset, weight_grad, bias_grad.reshape(COLS),
        gens_grad.reshape(4, 32, 1024), center_grad,
    )


def solution(mesh):
    return jax.shard_map(
        body,
        mesh=mesh,
        in_specs=(
            P("box", "gen", None),
            P("box", None),
            P("gen", "neur"),
            P("neur"),
            P("box", "neur"),
            P("box", "gen", "neur"),
            P("box", "neur"),
            P("box", "neur"),
        ),
        out_specs=(
            P("box", "neur"),
            P("box", "gen", "neur"),
            P("box", "neur"),
            P("gen", "neur"),
            P("neur"),
            P("box", "gen", "neur"),
            P("box", "neur"),
        ),
        check_vma=False,
    )
```

time: 407 us -> 78.6 us (0.19)
  the two profiles are of different devices: /device:TPU:1 before, /device:TPU:2 now
where the time goes in v1:
time: 78.6 us; the launch traced here: 78.4 us
  Pallas kernels  69.8 us (89%)
  local copies, waits for them, and re-layouts  7.87 us (10%)
    pallas_call x1, Pallas kernels, body(): pl.pallas_call(kernel, out_shape=(sds((4, COLS), F32), sds((ROWS, COLS),...  69.8 us
    unnamed x13, local copies, waits for them, and re-layouts  7.87 us

profile of v1, /device:TPU:2, one launch (start us, length us, event | category | flops | bytes accessed | tf_op | source)
XLA Modules:
  0.0 78.4 jit_solution(7402782134576723696)
XLA Ops:
  0.6 69.8 %zonotope_step.1 = (f32[4,512]{1,0:T(4,128)}, bf16[128,512]{1,0:T(8,128)(2,1)}, f32[4,512]{1,0:T(4,128)}, f32[128,512]{1,0:T(8,128)}, f32[1,512]{1,0:T(1,128)}, /*index=5*/f32[128,1024]{1,0:T(8,128)}, f32[4,1024]{1,0:T(4,128)}) custom-call(bf16[128,4096]{1,0:T(8,128)(2,1)} %bitcast.6, bf16[4,4096]{1,0:T(4,128)(2,1)} %center_ref.1, bf16[128,512]{1,0:T(8,128)(2,1)} %w_hbm.1, ...), custom_call_target="tpu_custom_call" | custom-call | tf_op jit(solution)/shard_map/zonotope_step/pallas_call | solution.py:393
  70.5 0.0 copy-start
  70.5 1.4 %copy.22 = f32[4,512]{1,0:T(4,128)} copy(f32[4,512]{1,0:T(4,128)} %get-tuple-element.28) | data formatting | bytes 16384
  71.8 1.6 %copy.23 = bf16[4,32,512]{2,1,0:T(8,128)(2,1)} copy(bf16[4,32,512]{2,1,0:T(8,128)(2,1)} %bitcast.8) | data formatting | bytes 262144
  73.4 1.3 %copy.24 = f32[4,512]{1,0:T(4,128)} copy(f32[4,512]{1,0:T(4,128)} %get-tuple-element.30) | data formatting | bytes 16384
  74.7 0.0 copy-start.2
  74.7 1.7 %copy.25 = f32[128,512]{1,0:T(8,128)} copy(f32[128,512]{1,0:T(8,128)} %get-tuple-element.31) | data formatting | bytes 524288
  76.4 0.0 copy-done.2
  76.4 0.6 copy.26
  76.9 0.0 copy-done
  77.0 0.0 copy-start.1
  77.0 0.8 %copy.27 = f32[4,32,1024]{2,1,0:T(8,128)} copy(f32[4,32,1024]{2,1,0:T(8,128)S(1)} %bitcast.7) | data formatting | bytes 1048576
  77.7 0.0 copy-done.1
  77.7 0.6 copy.28
Async XLA Ops:
  70.5 6.5 %copy-start = (f32[128,1024]{1,0:T(8,128)S(1)}, f32[128,1024]{1,0:T(8,128)}, u32[]{:S(2)}) copy-start(f32[128,1024]{1,0:T(8,128)} %get-tuple-element.19) | copy-start | bytes 1572868
  74.7 1.7 %copy-start.2 = (f32[1,512]{1,0:T(1,128)S(1)}, f32[1,512]{1,0:T(1,128)}, u32[]{:S(2)}) copy-start(f32[1,512]{1,0:T(1,128)} %get-tuple-element.18) | copy-start | bytes 6148
  77.0 0.8 %copy-start.1 = (f32[4,1024]{1,0:T(4,128)S(1)}, f32[4,1024]{1,0:T(4,128)}, u32[]{:S(2)}) copy-start(f32[4,1024]{1,0:T(4,128)} %get-tuple-element.34) | copy-start | bytes 49156

commit v2 on v0

v2 whole, which is shorter than its diff:
```python
import math

import jax
import jax.numpy as jnp
from jax import lax
from jax.experimental import pallas as pl
from jax.experimental.pallas import tpu as pltpu
from jax.sharding import PartitionSpec as P

MESH = pl.DeviceIdType.MESH
F32 = jnp.float32
BF16 = jnp.bfloat16

NZ = 8
D = 4096
COLS = 512
ROWS = 128
WIDE = 144
NH = 4
PIECE = 128 // NH
HALF = NH // 2
NP = 2
FP = COLS // NP


def neuron(center_pre, radius, phase):
    upper = center_pre + radius
    lower = center_pre - radius
    ratio = jnp.clip(upper / (upper - lower + 1e-05), 0.0, 1.0)
    active = (phase == 1).astype(center_pre.dtype)
    crossing = (phase == 2).astype(center_pre.dtype)
    slope = active + crossing * ratio
    offset = crossing * (-ratio * lower * 0.5)
    return (slope, slope * center_pre + offset, offset)


def zsteps(d):
    return {0: (0,), 4: (4,)}.get(d, (-d, d))


def kernel(
    gens_hbm, center_hbm, w_hbm, bias_hbm, phase_hbm, cot_hbm, ccot_hbm, ocot_hbm,
    cout_ref, gout_ref, off_ref, wg_ref, bg_ref, gg_ref, cg_ref,
    center_ref, bias_ref, phase_ref, cot_ref, ccot_ref, ocot_ref,
    w, wide, acc, cslot, gt, amat, sa, sb, bk, bmat, cmat, zs, zr, gs, gr, fx, xb,
    load_sem, out_sem, wz_sem, wy_sem, wp_sem, a_sem, s_sem, bo_sem, bf_sem, bp_sem, z_sem, f_sem, gx_sem,
):
    me = lax.axis_index("gen")
    x = lax.axis_index("neur")
    yhi = lax.axis_index("box")
    z = me // 4
    ylo = (me // 2) % 2
    c = me % 2
    y = yhi * 2 + ylo
    quad = ylo * 2 + c

    def dev(zz, yy, cc, xx=None):
        return (zz * 4 + (yy % 2) * 2 + cc, x if xx is None else xx, yy // 2)

    def zdev(k):
        return dev((z + NZ + k) % NZ, y, c)

    def ydev(k, cc=None):
        return dev(z, (y + k) % 4, c if cc is None else cc)

    def xdev(k):
        return dev(z, y, c, (x + k) % 4)

    partner = dev(z, y, 1 - c)
    other_box = ydev(2)

    sent = [0, 0, 0]

    def copy_to(src, dst, group, recv_sem, device):
        return pltpu.make_async_remote_copy(
            src_ref=src,
            dst_ref=dst,
            send_sem=out_sem.at[group],
            recv_sem=recv_sem,
            device_id=device,
            device_id_type=MESH,
        )

    def go(src, dst, group, recv_sem, device):
        copy_to(src, dst, group, recv_sem, device).start()
        sent[group] += math.prod(src.shape) * src.dtype.itemsize

    def await_bytes(ref, recv_sem):
        copy_to(ref, ref, 0, recv_sem, partner).wait_recv()

    barrier = pltpu.get_barrier_semaphore()
    peers = [partner, zdev(1), zdev(-1)] + [xdev(k) for k in (1, 2, 3)]
    peers += [ydev(k, cc) for k in (1, 2, 3) for cc in (0, 1)]
    for peer in peers:
        pl.semaphore_signal(barrier, inc=1, device_id=peer, device_id_type=MESH)

    loads = [
        pltpu.make_async_copy(src, dst, load_sem.at[i])
        for i, (src, dst) in enumerate(
            (
                (gens_hbm, wide.at[pl.ds(0, ROWS)]),
                (center_hbm, center_ref),
                (w_hbm, w.at[pl.ds(pl.multiple_of(me * 128, 128), 128)]),
                (bias_hbm, bias_ref),
                (phase_hbm, phase_ref),
                (cot_hbm, cot_ref),
                (ccot_hbm, ccot_ref),
                (ocot_hbm, ocot_ref),
            )
        )
    ]
    for cp in loads:
        cp.start()
    pl.semaphore_wait(barrier, len(peers))

    def chunk(zz, yl, cc, h=0, n=NH):
        at = (zz * 4 + yl * 2 + cc) * 128 + h * PIECE
        return w.at[pl.ds(pl.multiple_of(at, PIECE), n * PIECE)]

    def send_z(way, zz, h, own=False):
        ref = chunk(zz, ylo, c, h, 1)
        src = w_hbm.at[h * PIECE : h * PIECE + PIECE] if own else ref
        go(src, ref, 0, wz_sem.at[zz, h], zdev(1) if way == 0 else zdev(-1))

    def send_y(zz, h, n, own=False):
        ref = chunk(zz, ylo, c, h, n)
        src = w_hbm.at[h * PIECE : (h + n) * PIECE] if own else ref
        go(src, ref, 0, wy_sem.at[zz], ydev(1) if h < HALF else ydev(3))

    def send_p(zz, yl, own=False):
        ref = chunk(zz, yl, c)
        go(w_hbm if own else ref, ref, 0, wp_sem.at[zz], partner)

    for h in range(NH):
        send_z(0, z, h, own=True)
        send_z(1, z, NH - 1 - h, own=True)
    send_y(z, 0, HALF, own=True)
    send_y(z, HALF, HALF, own=True)
    send_p(z, ylo, own=True)

    loads[0].wait()

    def turn(i, carry):
        at = pl.multiple_of(i * 128, 128)
        gt[pl.ds(at, 128), :] = wide[0:ROWS, pl.ds(at, 128)].astype(F32).T.astype(BF16)
        return carry

    lax.fori_loop(8 * x, 8 * x + 8, turn, 0)
    gt3 = gt.reshape(NZ, 512, 128)

    def a_rows(yy, cc):
        return pl.ds(pl.multiple_of((yy % 2) * 256 + cc * 128 + (yy // 2) * 64, 64), 64)

    def lanes(at, n=128):
        return pl.ds(pl.multiple_of(at, 128), n)

    mine = pl.ds(2 * x, 2)
    for k in (2, 1, 3):
        r = 4 - k
        for cc in (0, 1):
            go(
                gt3.at[mine, a_rows((y + k) % 4, cc), :],
                amat.at[mine, :, lanes((r * 2 + c) * 128)],
                1,
                a_sem.at[0],
                ydev(k, cc),
            )

    loads[1].wait()
    wide[pl.ds(ROWS, 16)] = jnp.concatenate([center_ref[...].astype(F32), jnp.zeros((12, D), F32)], 0).astype(BF16)
    acc[...] = jnp.zeros_like(acc)
    lax.fori_loop(8 * x + 8, 8 * x + 32, lambda i, carry: turn(i % 32, carry), 0)
    own_a = pltpu.make_async_copy(gt3.at[:, a_rows(y, c), :], amat.at[:, :, lanes(c * 128)], load_sem.at[8])
    own_a.start()
    for cp in loads[2:]:
        cp.wait()

    def a_spread():
        ref = amat.at[mine, :, lanes(256, 768)]
        await_bytes(ref, a_sem.at[0])
        for k in (2, 1, 3):
            go(ref, ref, 1, a_sem.at[1], xdev(k))
        go(gt3.at[:, a_rows(y, 1 - c), :], amat.at[:, :, lanes(c * 128)], 1, a_sem.at[2], partner)

    def handle_y(d):
        for dz in zsteps(d):
            zz = (z + NZ + dz) % NZ
            await_bytes(chunk(zz, 1 - ylo, c), wy_sem.at[zz])
            send_p(zz, 1 - ylo)

    def compute(d):
        for dz in zsteps(d):
            zz = (z + NZ + dz) % NZ
            await_bytes(chunk(zz, 0, 0, 0, 2 * NH), wp_sem.at[zz])
            at = pl.ds(pl.multiple_of(zz * 512, 512), 512)
            res = jnp.dot(wide[:, at], w[at, :], preferred_element_type=F32)
            acc[...] += res[:ROWS]
            cslot[zz] = res[ROWS : ROWS + 8]

    for d in (1, 2, 3, 4):
        for i in range(NH):
            for way in (0, 1):
                h = i if way == 0 else NH - 1 - i
                if d == 4 and i >= HALF:
                    continue
                zz = (z + NZ - d) % NZ if way == 0 else (z + d) % NZ
                await_bytes(chunk(zz, ylo, c, h, 1), wz_sem.at[zz, h])
                if d < 3 or (d == 3 and i < HALF):
                    send_z(way, zz, h)
                if d == 4:
                    send_y(zz, h, 1)
                elif i % HALF == HALF - 1:
                    send_y(zz, 0 if h < HALF else HALF, HALF)
        for dz in zsteps(d):
            send_p((z + NZ + dz) % NZ, ylo)
        if d >= 2:
            handle_y(d - 2)
        if d == 2:
            a_spread()
        if d >= 3:
            compute(d - 3)
    handle_y(3)
    compute(2)
    handle_y(4)
    compute(3)
    compute(4)

    gen_pre = acc[...]
    cot = cot_ref[...].astype(F32)
    part_radius = jnp.sum(jnp.abs(gen_pre).reshape(4, 32, COLS), axis=1)
    part_inner = jnp.sum((cot * gen_pre).reshape(4, 32, COLS), axis=1)
    sa[quad] = jnp.concatenate([part_radius, part_inner], 0)
    for k in (1, 2, 3):
        go(sa.at[quad], sa.at[quad], 1, s_sem.at[0], (z * 4 + (quad + k) % 4, x, yhi))
    await_bytes(sa.at[pl.ds(0, 3)], s_sem.at[0])
    sb[z] = (sa[0] + sa[1]) + (sa[2] + sa[3])
    for k in (4, 3, 5, 2, 6, 1, 7):
        go(sb.at[z], sb.at[z], 1, s_sem.at[1], zdev(k))
    center_pre = cslot[0][0:4]
    for i in range(1, NZ):
        center_pre = center_pre + cslot[i][0:4]
    center_pre = center_pre + bias_ref[...]
    await_bytes(sb.at[pl.ds(0, NZ - 1)], s_sem.at[1])
    total = ((sb[0] + sb[1]) + (sb[2] + sb[3])) + ((sb[4] + sb[5]) + (sb[6] + sb[7]))
    radius = total[0:4]
    intersection = total[4:8]

    phase = phase_ref[...]
    (slope, center_out, offset), pull = jax.vjp(lambda a, b: neuron(a, b, phase), center_pre, radius)
    g_center, g_radius = pull((intersection, ccot_ref[...], ocot_ref[...]))
    pre3 = gen_pre.reshape(4, 32, COLS)
    sign = jnp.where(pre3 > 0, 1.0, jnp.where(pre3 < 0, -1.0, 0.0))
    back = (slope[:, None, :] * cot.reshape(4, 32, COLS) + sign * g_radius[:, None, :]).astype(BF16).reshape(ROWS, COLS)
    bk[0:ROWS] = back
    bmat[pl.ds(pl.multiple_of(c * 128, 128), 128)] = back

    def b_part(r, cc, p, i=0, n=64):
        return bmat.at[pl.ds(pl.multiple_of((r * 2 + cc) * 128 + i * 64, 64), n), pl.ds(p * FP, FP)]

    def bk_part(p, i=0, n=64):
        return bk.at[i * 64 : i * 64 + n, pl.ds(p * FP, FP)]

    for p in range(NP):
        for i in (0, 1):
            j = 1 - i
            go(bk_part(p, i), b_part(3, c, p, i), 2, bo_sem.at[0, i, p], ydev(1))
            go(bk_part(p, j), b_part(1, c, p, j), 2, bo_sem.at[1, j, p], ydev(3))
        go(bk_part(p, 0, 128), b_part(0, c, p, 0, 128), 2, bp_sem.at[0, p], partner)

    center_back = g_center.astype(BF16).astype(F32)
    bk[pl.ds(ROWS, 16)] = jnp.concatenate([center_back, jnp.zeros((12, COLS), F32)], 0).astype(BF16)
    xb[yhi, :, 0:COLS] = jnp.concatenate([center_back, jnp.sum(g_center, axis=0, keepdims=True), jnp.zeros((3, COLS), F32)], 0)
    xb[yhi, :, COLS:] = jnp.concatenate(
        [
            jnp.concatenate([center_ref[:, lanes(me * 128)].astype(F32), jnp.zeros((4, 128), F32)], 0),
            jnp.zeros((8, COLS - 128), F32),
        ],
        1,
    )
    go(xb.at[yhi], xb.at[yhi], 2, gx_sem.at[1], other_box)

    def partial(k):
        at = pl.ds(pl.multiple_of(((x + k) % 4) * 1024, 1024), 1024)
        return lax.dot_general(bk[...], w[at, :], (((1,), (1,)), ((), ())), preferred_element_type=F32)

    for k in (2, 1, 3):
        gs[k - 1] = partial(k).astype(BF16)
        go(gs.at[k - 1], gr.at[3 - k], 2, gx_sem.at[0], xdev(k))

    cout_ref[...] = center_out
    off_ref[...] = offset
    gout_ref[...] = (slope[:, None, :] * pre3).astype(BF16).reshape(ROWS, COLS)

    own_a.wait()
    spread = gt.at[pl.ds(0, 3 * 2 * 64 * 6)]
    await_bytes(spread, a_sem.at[1])
    await_bytes(amat.at[:, :, lanes((1 - c) * 128)], a_sem.at[2])

    def b_forward(p):
        for i in (0, 1):
            for r, h, to in ((3, i, 1), (1, 1 - i, 3)):
                await_bytes(b_part(r, c, p, h), bo_sem.at[0 if r == 3 else 1, h, p])
                if i == 0:
                    go(b_part(r, c, p, h), b_part(2, c, p, h), 2, bf_sem.at[p], ydev(to))
        for r in (3, 1):
            go(b_part(r, c, p, 0, 128), b_part(r, c, p, 0, 128), 2, bp_sem.at[r, p], partner)

    def b_last(p):
        ref = b_part(2, c, p, 0, 128)
        await_bytes(ref, bf_sem.at[p])
        go(ref, ref, 2, bp_sem.at[2, p], partner)

    def c_pass(r, p):
        await_bytes(b_part(r, 1 - c, p, 0, 128), bp_sem.at[r, p])
        a = amat[:, :, r * 256 : r * 256 + 256].reshape(512, 256)
        cols = pl.ds(p * FP, FP)
        res = jnp.dot(a, bmat[r * 256 : r * 256 + 256, cols], preferred_element_type=F32).reshape(NZ, 64, FP)
        if r == 0:
            cmat[:, :, cols] = res
        else:
            cmat[:, :, cols] += res

    def z_step(dist, p):
        for way in (0, 1):
            longest = 4 if p % 2 == way else 3
            if dist > longest:
                continue
            val = cmat[(z + NZ + (dist if way == 0 else -dist)) % NZ, :, pl.ds(p * FP, FP)]
            if dist < longest:
                await_bytes(zr.at[way, dist, p], z_sem.at[way, dist, p])
                val = val + zr[way, dist, p].astype(F32)
            if dist > 0:
                zs[way, dist, p] = val.astype(BF16)
                to = zdev(1 if way == 0 else -1)
                go(zs.at[way, dist, p], zr.at[way, dist - 1, p], 2, z_sem.at[way, dist - 1, p], to)
            elif way == 1:
                val = val + zr[0, 0, p].astype(F32)
                fx[yhi, p] = val.astype(BF16)
                go(fx.at[yhi, p], fx.at[yhi, p], 2, f_sem.at[p], other_box)

    for p in range(NP):
        b_forward(p)
    for p in range(NP):
        for r in (0, 3, 1):
            c_pass(r, p)
        b_last(p)
        c_pass(2, p)
        z_step(4, p)
        if p > 0:
            z_step(3, p - 1)
    z_step(3, NP - 1)
    own = partial(0)
    for dist in (2, 1, 0):
        for p in range(NP):
            z_step(dist, p)

    await_bytes(gr, gx_sem.at[0])
    summed = own + gr[0].astype(F32) + gr[1].astype(F32) + gr[2].astype(F32)
    gg_ref[...] = summed[:ROWS]
    cg_ref[...] = summed[ROWS : ROWS + 4]

    other = 1 - yhi
    await_bytes(xb.at[other], gx_sem.at[1])
    xall = xb[:, :, 0 : COLS + 128].reshape(16, COLS + 128)
    term = lax.dot_general(
        xall[:, COLS:].T.astype(BF16), xall[:, :COLS].astype(BF16), (((1,), (0,)), ((), ())), preferred_element_type=F32
    )
    bg_ref[...] = xall[4:5, :COLS] + xall[12:13, :COLS]
    for p in range(NP):
        await_bytes(fx.at[other, p], f_sem.at[p])
        at = p * FP
        wg_ref[:, at : at + FP] = fx[:, p].astype(F32).reshape(128, FP) + term[:, at : at + FP]

    for group, count in enumerate(sent):
        ref = w.at[pl.ds(0, count // (COLS * 2))]
        copy_to(ref, ref, group, out_sem.at[group], partner).wait_send()


def finish(*refs):
    for src, dst in zip(refs[:7], refs[7:]):
        dst[...] = src[...]


def body(gens, center, weight, bias, phase, gens_cot, center_cot, offset_cot):
    vm = pl.BlockSpec(memory_space=pltpu.VMEM)
    hbm = pl.BlockSpec(memory_space=pltpu.HBM)
    dma = pltpu.SemaphoreType.DMA
    sds = jax.ShapeDtypeStruct
    outs = pl.pallas_call(
        kernel,
        out_shape=(
            sds((4, COLS), F32),
            sds((ROWS, COLS), BF16),
            sds((4, COLS), F32),
            sds((128, COLS), F32),
            sds((1, COLS), F32),
            sds((ROWS, 1024), F32),
            sds((4, 1024), F32),
        ),
        in_specs=[hbm] * 8,
        out_specs=(vm,) * 7,
        scratch_shapes=[
            pltpu.VMEM((4, D), BF16),
            pltpu.VMEM((1, COLS), F32),
            pltpu.VMEM((4, COLS), jnp.int32),
            pltpu.VMEM((ROWS, COLS), BF16),
            pltpu.VMEM((4, COLS), F32),
            pltpu.VMEM((4, COLS), F32),
            pltpu.VMEM((D, COLS), BF16),
            pltpu.VMEM((WIDE, D), BF16),
            pltpu.VMEM((ROWS, COLS), F32),
            pltpu.VMEM((NZ, 8, COLS), F32),
            pltpu.VMEM((D, ROWS), BF16),
            pltpu.VMEM((NZ, 64, 1024), BF16),
            pltpu.VMEM((4, 8, COLS), F32),
            pltpu.VMEM((NZ, 8, COLS), F32),
            pltpu.VMEM((WIDE, COLS), BF16),
            pltpu.VMEM((1024, COLS), BF16),
            pltpu.VMEM((NZ, 64, COLS), F32),
            pltpu.VMEM((2, 5, NP, 64, FP), BF16),
            pltpu.VMEM((2, 5, NP, 64, FP), BF16),
            pltpu.VMEM((3, WIDE, 1024), BF16),
            pltpu.VMEM((3, WIDE, 1024), BF16),
            pltpu.VMEM((2, NP, 64, FP), BF16),
            pltpu.VMEM((2, 8, 2 * COLS), F32),
            dma((9,)),
            dma((3,)),
            dma((NZ, NH)),
            dma((NZ,)),
            dma((NZ,)),
            dma((3,)),
            dma((2,)),
            dma((2, 2, NP)),
            dma((NP,)),
            dma((4, NP)),
            dma((2, 4, NP)),
            dma((NP,)),
            dma((2,)),
        ],
        compiler_params=pltpu.CompilerParams(
            collective_id=0, has_side_effects=True, vmem_limit_bytes=32 * 1024 * 1024
        ),
        name="zonotope_step",
    )(
        *(
            pltpu.with_memory_space_constraint(v, pltpu.HBM)
            for v in (
                gens.reshape(ROWS, D), center, weight, bias.reshape(1, COLS), phase,
                gens_cot.reshape(ROWS, COLS), center_cot, offset_cot,
            )
        )
    )
    outs = pl.pallas_call(
        finish,
        out_shape=tuple(sds(o.shape, o.dtype) for o in outs),
        in_specs=[vm] * 7,
        out_specs=(vm,) * 7,
        compiler_params=pltpu.CompilerParams(vmem_limit_bytes=8 * 1024 * 1024),
        name="finish",
    )(*outs)
    center_out, gens_out, offset, weight_grad, bias_grad, gens_grad, center_grad = outs
    return (
        center_out, gens_out.reshape(4, 32, COLS), offset, weight_grad, bias_grad.reshape(COLS),
        gens_grad.reshape(4, 32, 1024), center_grad,
    )


def solution(mesh):
    return jax.shard_map(
        body,
        mesh=mesh,
        in_specs=(
            P("box", "gen", None),
            P("box", None),
            P("gen", "neur"),
            P("neur"),
            P("box", "neur"),
            P("box", "gen", "neur"),
            P("box", "neur"),
            P("box", "neur"),
        ),
        out_specs=(
            P("box", "neur"),
            P("box", "gen", "neur"),
            P("box", "neur"),
            P("gen", "neur"),
            P("neur"),
            P("box", "gen", "neur"),
            P("box", "neur"),
        ),
        check_vma=False,
    )
```

time: 407 us -> 63.8 us (0.16)
  the two profiles are of different devices: /device:TPU:1 before, /device:TPU:32 now
where the time goes in v2:
time: 63.8 us; the launch traced here: 63.7 us
  Pallas kernels  63.1 us (99%)
  between operations  0.64 us (1%)
    pallas_call x1, Pallas kernels, body(): pl.pallas_call(kernel, out_shape=(sds((4, COLS), F32), sds((ROWS, COLS),...  62.1 us

profile of v2, /device:TPU:32, one launch (start us, length us, event | category | flops | bytes accessed | tf_op | source)
XLA Modules:
  0.0 63.7 jit_solution(9373366961694951134)
XLA Ops:
  0.6 62.1 %zonotope_step.1 = (f32[4,512]{1,0:T(4,128)S(1)}, bf16[128,512]{1,0:T(8,128)(2,1)S(1)}, f32[4,512]{1,0:T(4,128)S(1)}, f32[128,512]{1,0:T(8,128)S(1)}, f32[1,512]...) custom-call(bf16[128,4096]{1,0:T(8,128)(2,1)} %bitcast.6, bf16[4,4096]{1,0:T(4,128)(2,1)} %center_hbm.1, ...), custom_call_target="tpu_custom_call" | custom-call | tf_op jit(solution)/shard_map/zonotope_step/pallas_call | solution.py:389
  62.7 1.0 %finish.1 = (f32[4,512]{1,0:T(4,128)}, bf16[128,512]{1,0:T(8,128)(2,1)}, f32[4,512]{1,0:T(4,128)}, f32[128,512]{1,0:T(8,128)}, f32[1,512]{1,0:T(1,128)}, /*index=5*/f32[128,1024]{1,0:T(8,128)}, f32[4,1024]{1,0:T(4,128)}) custom-call(f32[4,512]{1,0:T(4,128)S(1)} %get-tuple-element.21.refs_0_, bf16[128,512]{1,0:T(8,128)(2,1)S(1)} %get-tuple-element.22.refs_1_, ...), custom_call_target="tpu_custom_call" | custom-call | tf_op jit(solution)/shard_map/finish/pallas_call | solution.py:453

commit v3 on v2

--- a/solution.py
+++ b/solution.py
@@ -19,8 +19,8 @@
 NH = 4
 PIECE = 128 // NH
 HALF = NH // 2
-NP = 2
-FP = COLS // NP
+NQ = 2
+FQ = COLS // NQ
 
 
 def neuron(center_pre, radius, phase):
@@ -41,9 +41,9 @@
 def kernel(
     gens_hbm, center_hbm, w_hbm, bias_hbm, phase_hbm, cot_hbm, ccot_hbm, ocot_hbm,
     cout_ref, gout_ref, off_ref, wg_ref, bg_ref, gg_ref, cg_ref,
-    center_ref, bias_ref, phase_ref, cot_ref, ccot_ref, ocot_ref,
-    w, wide, acc, cslot, gt, amat, sa, sb, bk, bmat, cmat, zs, zr, gs, gr, fx, xb,
-    load_sem, out_sem, wz_sem, wy_sem, wp_sem, a_sem, s_sem, bo_sem, bf_sem, bp_sem, z_sem, f_sem, gx_sem,
+    center_ref, bias_ref, phase_ref, ccot_ref, ocot_ref,
+    w, wide, acc, cslot, gt, amat, sa, sb, bk, call, sall, xs, cmat, zs, zr, gs, gr, fx, xb,
+    load_sem, out_sem, wz_sem, wy_sem, wp_sem, a_sem, s_sem, near_sem, far_sem, pair_sem, f_sem, gx_sem,
 ):
     me = lax.axis_index("gen")
     x = lax.axis_index("neur")
@@ -103,7 +103,7 @@
                 (w_hbm, w.at[pl.ds(pl.multiple_of(me * 128, 128), 128)]),
                 (bias_hbm, bias_ref),
                 (phase_hbm, phase_ref),
-                (cot_hbm, cot_ref),
+                (cot_hbm, call.at[pl.ds(pl.multiple_of(c * 128, 128), 128)]),
                 (ccot_hbm, ccot_ref),
                 (ocot_hbm, ocot_ref),
             )
@@ -196,6 +196,32 @@
             res = jnp.dot(wide[:, at], w[at, :], preferred_element_type=F32)
             acc[...] += res[:ROWS]
             cslot[zz] = res[ROWS : ROWS + 8]
+
+    held = (call, sall)
+
+    def part(b, r, cc, i=0, n=64):
+        return held[b].at[pl.ds(pl.multiple_of((r * 2 + cc) * 128 + i * 64, 64), n)]
+
+    def gather_own(b):
+        for i in (0, 1):
+            j = 1 - i
+            go(part(b, 0, c, i), part(b, 3, c, i), 2, near_sem.at[b, i], ydev(1))
+            go(part(b, 0, c, j), part(b, 1, c, j), 2, near_sem.at[b, 2 + j], ydev(3))
+        go(part(b, 0, c, 0, 128), part(b, 0, c, 0, 128), 2, pair_sem.at[b, 0], partner)
+
+    def gather_forward(b):
+        for i in (0, 1):
+            for r, h, to in ((3, i, 1), (1, 1 - i, 3)):
+                await_bytes(part(b, r, c, h), near_sem.at[b, h if r == 3 else 2 + h])
+                if i == 0:
+                    go(part(b, r, c, h), part(b, 2, c, h), 2, far_sem.at[b], ydev(to))
+        for r in (3, 1):
+            go(part(b, r, c, 0, 128), part(b, r, c, 0, 128), 2, pair_sem.at[b, r], partner)
+
+    def gather_last(b):
+        ref = part(b, 2, c, 0, 128)
+        await_bytes(ref, far_sem.at[b])
+        go(ref, ref, 2, pair_sem.at[b, 2], partner)
 
     for d in (1, 2, 3, 4):
         for i in range(NH):
@@ -213,6 +239,8 @@
                     send_y(zz, 0 if h < HALF else HALF, HALF)
         for dz in zsteps(d):
             send_p((z + NZ + dz) % NZ, ylo)
+        if d == 4:
+            gather_own(0)
         if d >= 2:
             handle_y(d - 2)
         if d == 2:
@@ -226,12 +254,16 @@
     compute(4)
 
     gen_pre = acc[...]
-    cot = cot_ref[...].astype(F32)
+    cot = call[pl.ds(pl.multiple_of(c * 128, 128), 128)].astype(F32)
     part_radius = jnp.sum(jnp.abs(gen_pre).reshape(4, 32, COLS), axis=1)
     part_inner = jnp.sum((cot * gen_pre).reshape(4, 32, COLS), axis=1)
     sa[quad] = jnp.concatenate([part_radius, part_inner], 0)
     for k in (1, 2, 3):
         go(sa.at[quad], sa.at[quad], 1, s_sem.at[0], (z * 4 + (quad + k) % 4, x, yhi))
+    pre3 = gen_pre.reshape(4, 32, COLS)
+    sign = jnp.where(pre3 > 0, 1.0, jnp.where(pre3 < 0, -1.0, 0.0))
+    sall[pl.ds(pl.multiple_of(c * 128, 128), 128)] = sign.reshape(ROWS, COLS).astype(BF16)
+    gather_own(1)
     await_bytes(sa.at[pl.ds(0, 3)], s_sem.at[0])
     sb[z] = (sa[0] + sa[1]) + (sa[2] + sa[3])
     for k in (4, 3, 5, 2, 6, 1, 7):
@@ -240,6 +272,9 @@
     for i in range(1, NZ):
         center_pre = center_pre + cslot[i][0:4]
     center_pre = center_pre + bias_ref[...]
+    gather_forward(0)
+    gather_forward(1)
+    gather_last(0)
     await_bytes(sb.at[pl.ds(0, NZ - 1)], s_sem.at[1])
     total = ((sb[0] + sb[1]) + (sb[2] + sb[3])) + ((sb[4] + sb[5]) + (sb[6] + sb[7]))
     radius = total[0:4]
@@ -248,24 +283,10 @@
     phase = phase_ref[...]
     (slope, center_out, offset), pull = jax.vjp(lambda a, b: neuron(a, b, phase), center_pre, radius)
     g_center, g_radius = pull((intersection, ccot_ref[...], ocot_ref[...]))
-    pre3 = gen_pre.reshape(4, 32, COLS)
-    sign = jnp.where(pre3 > 0, 1.0, jnp.where(pre3 < 0, -1.0, 0.0))
     back = (slope[:, None, :] * cot.reshape(4, 32, COLS) + sign * g_radius[:, None, :]).astype(BF16).reshape(ROWS, COLS)
     bk[0:ROWS] = back
-    bmat[pl.ds(pl.multiple_of(c * 128, 128), 128)] = back
-
-    def b_part(r, cc, p, i=0, n=64):
-        return bmat.at[pl.ds(pl.multiple_of((r * 2 + cc) * 128 + i * 64, 64), n), pl.ds(p * FP, FP)]
-
-    def bk_part(p, i=0, n=64):
-        return bk.at[i * 64 : i * 64 + n, pl.ds(p * FP, FP)]
-
-    for p in range(NP):
-        for i in (0, 1):
-            j = 1 - i
-            go(bk_part(p, i), b_part(3, c, p, i), 2, bo_sem.at[0, i, p], ydev(1))
-            go(bk_part(p, j), b_part(1, c, p, j), 2, bo_sem.at[1, j, p], ydev(3))
-        go(bk_part(p, 0, 128), b_part(0, c, p, 0, 128), 2, bp_sem.at[0, p], partner)
+    xs[yhi] = jnp.concatenate([slope, g_radius], 0)
+    go(xs.at[yhi], xs.at[yhi], 2, gx_sem.at[2], ydev(3 - 2 * ylo))
 
     center_back = g_center.astype(BF16).astype(F32)
     bk[pl.ds(ROWS, 16)] = jnp.concatenate([center_back, jnp.zeros((12, COLS), F32)], 0).astype(BF16)
@@ -283,76 +304,75 @@
         at = pl.ds(pl.multiple_of(((x + k) % 4) * 1024, 1024), 1024)
         return lax.dot_general(bk[...], w[at, :], (((1,), (1,)), ((), ())), preferred_element_type=F32)
 
-    for k in (2, 1, 3):
+    def g_start(k):
         gs[k - 1] = partial(k).astype(BF16)
         go(gs.at[k - 1], gr.at[3 - k], 2, gx_sem.at[0], xdev(k))
 
+    def have(r):
+        for b in (0, 1):
+            await_bytes(part(b, r, 1 - c, 0, 128), pair_sem.at[b, r])
+
+    def c_pass(r, box, at, n, first=False):
+        cols = pl.ds(at, n)
+        rows = pl.ds(pl.multiple_of(r * 256, 256), 256)
+        scale = xs[box, 0:4, cols][None, :, None, :]
+        g_rad = xs[box, 4:8, cols][None, :, None, :]
+        cots = call[rows, cols].astype(F32).reshape(2, 4, 32, n)
+        signs = sall[rows, cols].astype(F32).reshape(2, 4, 32, n)
+        back = (scale * cots + signs * g_rad).astype(BF16).reshape(256, n)
+        a = amat[:, :, lanes(r * 256, 256)].reshape(512, 256)
+        res = jnp.dot(a, back, preferred_element_type=F32).reshape(NZ, 64, n)
+        if first:
+            cmat[:, :, cols] = res
+        else:
+            cmat[:, :, cols] += res
+
+    g_start(2)
+    own_a.wait()
+    await_bytes(gt.at[pl.ds(0, 3 * 2 * 64 * 6)], a_sem.at[1])
+    await_bytes(amat.at[:, :, lanes((1 - c) * 128)], a_sem.at[2])
+    gather_last(1)
+    have(0)
+    c_pass(0, yhi, 0, COLS, first=True)
+    g_start(1)
+    have(3)
+    have(1)
+    c_pass(1 + 2 * ylo, yhi, 0, COLS)
+    g_start(3)
     cout_ref[...] = center_out
     off_ref[...] = offset
     gout_ref[...] = (slope[:, None, :] * pre3).astype(BF16).reshape(ROWS, COLS)
-
-    own_a.wait()
-    spread = gt.at[pl.ds(0, 3 * 2 * 64 * 6)]
-    await_bytes(spread, a_sem.at[1])
-    await_bytes(amat.at[:, :, lanes((1 - c) * 128)], a_sem.at[2])
-
-    def b_forward(p):
-        for i in (0, 1):
-            for r, h, to in ((3, i, 1), (1, 1 - i, 3)):
-                await_bytes(b_part(r, c, p, h), bo_sem.at[0 if r == 3 else 1, h, p])
-                if i == 0:
-                    go(b_part(r, c, p, h), b_part(2, c, p, h), 2, bf_sem.at[p], ydev(to))
-        for r in (3, 1):
-            go(b_part(r, c, p, 0, 128), b_part(r, c, p, 0, 128), 2, bp_sem.at[r, p], partner)
-
-    def b_last(p):
-        ref = b_part(2, c, p, 0, 128)
-        await_bytes(ref, bf_sem.at[p])
-        go(ref, ref, 2, bp_sem.at[2, p], partner)
-
-    def c_pass(r, p):
-        await_bytes(b_part(r, 1 - c, p, 0, 128), bp_sem.at[r, p])
-        a = amat[:, :, r * 256 : r * 256 + 256].reshape(512, 256)
-        cols = pl.ds(p * FP, FP)
-        res = jnp.dot(a, bmat[r * 256 : r * 256 + 256, cols], preferred_element_type=F32).reshape(NZ, 64, FP)
-        if r == 0:
-            cmat[:, :, cols] = res
-        else:
-            cmat[:, :, cols] += res
-
-    def z_step(dist, p):
+    await_bytes(xs.at[1 - yhi], gx_sem.at[2])
+    c_pass(3 - 2 * ylo, 1 - yhi, 0, COLS)
+    have(2)
+
+    def z_step(dist, q):
         for way in (0, 1):
-            longest = 4 if p % 2 == way else 3
+            longest = 4 if q % 2 == way else 3
             if dist > longest:
                 continue
-            val = cmat[(z + NZ + (dist if way == 0 else -dist)) % NZ, :, pl.ds(p * FP, FP)]
+            val = cmat[(z + NZ + (dist if way == 0 else -dist)) % NZ, :, pl.ds(q * FQ, FQ)]
             if dist < longest:
-                await_bytes(zr.at[way, dist, p], z_sem.at[way, dist, p])
-                val = val + zr[way, dist, p].astype(F32)
+                await_bytes(zr.at[way, dist, q], wz_sem.at[way * 4 + dist, q])
+                val = val + zr[way, dist, q].astype(F32)
             if dist > 0:
-                zs[way, dist, p] = val.astype(BF16)
+                zs[way, dist, q] = val.astype(BF16)
                 to = zdev(1 if way == 0 else -1)
-                go(zs.at[way, dist, p], zr.at[way, dist - 1, p], 2, z_sem.at[way, dist - 1, p], to)
+                go(zs.at[way, dist, q], zr.at[way, dist - 1, q], 2, wz_sem.at[way * 4 + dist - 1, q], to)
             elif way == 1:
-                val = val + zr[0, 0, p].astype(F32)
-                fx[yhi, p] = val.astype(BF16)
-                go(fx.at[yhi, p], fx.at[yhi, p], 2, f_sem.at[p], other_box)
-
-    for p in range(NP):
-        b_forward(p)
-    for p in range(NP):
-        for r in (0, 3, 1):
-            c_pass(r, p)
-        b_last(p)
-        c_pass(2, p)
-        z_step(4, p)
-        if p > 0:
-            z_step(3, p - 1)
-    z_step(3, NP - 1)
+                val = val + zr[0, 0, q].astype(F32)
+                fx[yhi, q] = val.astype(BF16)
+                go(fx.at[yhi, q], fx.at[yhi, q], 2, f_sem.at[q], other_box)
+
+    for q in range(NQ):
+        c_pass(2, 1 - yhi, q * FQ, FQ)
+        z_step(4, q)
+    for q in range(NQ):
+        z_step(3, q)
     own = partial(0)
     for dist in (2, 1, 0):
-        for p in range(NP):
-            z_step(dist, p)
+        for q in range(NQ):
+            z_step(dist, q)
 
     await_bytes(gr, gx_sem.at[0])
     summed = own + gr[0].astype(F32) + gr[1].astype(F32) + gr[2].astype(F32)
@@ -366,10 +386,10 @@
         xall[:, COLS:].T.astype(BF16), xall[:, :COLS].astype(BF16), (((1,), (0,)), ((), ())), preferred_element_type=F32
     )
     bg_ref[...] = xall[4:5, :COLS] + xall[12:13, :COLS]
-    for p in range(NP):
-        await_bytes(fx.at[other, p], f_sem.at[p])
-        at = p * FP
-        wg_ref[:, at : at + FP] = fx[:, p].astype(F32).reshape(128, FP) + term[:, at : at + FP]
+    for q in range(NQ):
+        await_bytes(fx.at[other, q], f_sem.at[q])
+        at = q * FQ
+        wg_ref[:, at : at + FQ] = fx[:, q].astype(F32).reshape(128, FQ) + term[:, at : at + FQ]
 
     for group, count in enumerate(sent):
         ref = w.at[pl.ds(0, count // (COLS * 2))]
@@ -403,7 +423,6 @@
             pltpu.VMEM((4, D), BF16),
             pltpu.VMEM((1, COLS), F32),
             pltpu.VMEM((4, COLS), jnp.int32),
-            pltpu.VMEM((ROWS, COLS), BF16),
             pltpu.VMEM((4, COLS), F32),
             pltpu.VMEM((4, COLS), F32),
             pltpu.VMEM((D, COLS), BF16),
@@ -416,12 +435,14 @@
             pltpu.VMEM((NZ, 8, COLS), F32),
             pltpu.VMEM((WIDE, COLS), BF16),
             pltpu.VMEM((1024, COLS), BF16),
+            pltpu.VMEM((1024, COLS), BF16),
+            pltpu.VMEM((2, 8, COLS), F32),
             pltpu.VMEM((NZ, 64, COLS), F32),
-            pltpu.VMEM((2, 5, NP, 64, FP), BF16),
-            pltpu.VMEM((2, 5, NP, 64, FP), BF16),
+            pltpu.VMEM((2, 5, NQ, 64, FQ), BF16),
+            pltpu.VMEM((2, 5, NQ, 64, FQ), BF16),
             pltpu.VMEM((3, WIDE, 1024), BF16),
             pltpu.VMEM((3, WIDE, 1024), BF16),
-            pltpu.VMEM((2, NP, 64, FP), BF16),
+            pltpu.VMEM((2, NQ, 64, FQ), BF16),
             pltpu.VMEM((2, 8, 2 * COLS), F32),
             dma((9,)),
             dma((3,)),
@@ -430,12 +451,11 @@
             dma((NZ,)),
             dma((3,)),
             dma((2,)),
-            dma((2, 2, NP)),
-            dma((NP,)),
-            dma((4, NP)),
-            dma((2, 4, NP)),
-            dma((NP,)),
+            dma((2, 4)),
             dma((2,)),
+            dma((2, 4)),
+            dma((NQ,)),
+            dma((3,)),
         ],
         compiler_params=pltpu.CompilerParams(
             collective_id=0, has_side_effects=True, vmem_limit_bytes=32 * 1024 * 1024

time: 63.8 us -> 60 us (0.940)
  the two profiles are of different devices: /device:TPU:32 before, /device:TPU:2 now
where the time goes in v3:
time: 60 us
  Pallas kernels  59.3 us (99%)
  between operations  0.64 us (1%)
    pallas_call x1, Pallas kernels, body(): pl.pallas_call(kernel, out_shape=(sds((4, COLS), F32), sds((ROWS, COLS),...  58.3 us

profile of v3, /device:TPU:2, one launch (start us, length us, event | category | flops | bytes accessed | tf_op | source)
XLA Modules:
  0.0 60.0 jit_solution(16713835466113068095)
XLA Ops:
  0.6 58.3 %zonotope_step.1 = (f32[4,512]{1,0:T(4,128)S(1)}, bf16[128,512]{1,0:T(8,128)(2,1)S(1)}, f32[4,512]{1,0:T(4,128)S(1)}, f32[128,512]{1,0:T(8,128)S(1)}, f32[1,512]...) custom-call(bf16[128,4096]{1,0:T(8,128)(2,1)} %bitcast.6, bf16[4,4096]{1,0:T(4,128)(2,1)} %center_hbm.1, ...), custom_call_target="tpu_custom_call" | custom-call | tf_op jit(solution)/shard_map/zonotope_step/pallas_call | solution.py:409
  59.0 1.0 %finish.1 = (f32[4,512]{1,0:T(4,128)}, bf16[128,512]{1,0:T(8,128)(2,1)}, f32[4,512]{1,0:T(4,128)}, f32[128,512]{1,0:T(8,128)}, f32[1,512]{1,0:T(1,128)}, /*index=5*/f32[128,1024]{1,0:T(8,128)}, f32[4,1024]{1,0:T(4,128)}) custom-call(f32[4,512]{1,0:T(4,128)S(1)} %get-tuple-element.21.refs_0_, bf16[128,512]{1,0:T(8,128)(2,1)S(1)} %get-tuple-element.22.refs_1_, ...), custom_call_target="tpu_custom_call" | custom-call | tf_op jit(solution)/shard_map/finish/pallas_call | solution.py:473

commit v4 on v0

v4 whole, which is shorter than its diff:
```python
import math

import jax
import jax.numpy as jnp
from jax import lax
from jax.experimental import pallas as pl
from jax.experimental.pallas import tpu as pltpu
from jax.sharding import PartitionSpec as P

MESH = pl.DeviceIdType.MESH
F32 = jnp.float32
BF16 = jnp.bfloat16

NZ = 8
D = 4096
COLS = 512
ROWS = 128
WIDE = 144
NH = 4
PIECE = 256 // NH
HALF = NH // 2
NQ = 4
FQ = COLS // NQ


def neuron(center_pre, radius, phase):
    upper = center_pre + radius
    lower = center_pre - radius
    ratio = jnp.clip(upper / (upper - lower + 1e-05), 0.0, 1.0)
    active = (phase == 1).astype(center_pre.dtype)
    crossing = (phase == 2).astype(center_pre.dtype)
    slope = active + crossing * ratio
    offset = crossing * (-ratio * lower * 0.5)
    return (slope, slope * center_pre + offset, offset)


def zsteps(d):
    return {0: (0,), 4: (4,)}.get(d, (-d, d))


def kernel(
    gens_hbm, center_hbm, w_hbm, bias_hbm, phase_hbm, cot_hbm, ccot_hbm, ocot_hbm,
    cout_ref, gout_ref, off_ref, wg_ref, bg_ref, gg_ref, cg_ref,
    center_ref, bias_ref, phase_ref, ccot_ref, ocot_ref,
    w, wide, acc, cslot, gt, amat, sa, sb, tot, bk, call, sall, xs, cmat, zs, zr, gs, gi, gr, keep, gown, gc, fs, fx, xb,
    load_sem, out_sem, wz_sem, wy_sem, wp_sem, a_sem, s_sem, near_sem, far_sem, pair_sem, f_sem, gx_sem,
):
    me = lax.axis_index("gen")
    x = lax.axis_index("neur")
    yhi = lax.axis_index("box")
    z = me // 4
    ylo = (me // 2) % 2
    c = me % 2
    y = yhi * 2 + ylo
    quad = ylo * 2 + c

    def dev(zz, yy, cc, xx=None):
        return (zz * 4 + (yy % 2) * 2 + cc, x if xx is None else xx, yy // 2)

    def zdev(k, cc=1):
        return dev((z + NZ + k) % NZ, y, cc)

    def ydev(k, cc=1):
        return dev(z, (y + k) % 4, cc)

    def xdev(k, cc):
        return dev(z, y, cc, (x + k) % 4)

    partner = dev(z, y, 1 - c)

    sent = {0: [0, 0, 0, 0], 1: [0, 0, 0, 0]}
    roles = [0, 1]

    def copy_to(src, dst, group, recv_sem, device):
        return pltpu.make_async_remote_copy(
            src_ref=src,
            dst_ref=dst,
            send_sem=out_sem.at[group],
            recv_sem=recv_sem,
            device_id=device,
            device_id_type=MESH,
        )

    def go(src, dst, group, recv_sem, device):
        copy_to(src, dst, group, recv_sem, device).start()
        for role in roles:
            sent[role][group] += math.prod(src.shape) * src.dtype.itemsize

    def await_bytes(ref, recv_sem):
        copy_to(ref, ref, 0, recv_sem, partner).wait_recv()

    barrier = pltpu.get_barrier_semaphore()
    peers = [partner] + [zdev(k, cc) for k in (1, -1) for cc in (0, 1)]
    peers += [f(k, cc) for f in (xdev, ydev) for k in (1, 2, 3) for cc in (0, 1)]
    for peer in peers:
        pl.semaphore_signal(barrier, inc=1, device_id=peer, device_id_type=MESH)

    loads = [
        pltpu.make_async_copy(src, dst, load_sem.at[i])
        for i, (src, dst) in enumerate(
            (
                (gens_hbm, wide.at[pl.ds(0, ROWS)]),
                (center_hbm, center_ref),
                (w_hbm, w.at[pl.ds(pl.multiple_of(me * 128, 128), 128)]),
                (bias_hbm, bias_ref),
                (phase_hbm, phase_ref),
                (cot_hbm, call.at[pl.ds(pl.multiple_of(c * 128, 128), 128)]),
                (ccot_hbm, ccot_ref),
                (ocot_hbm, ocot_ref),
            )
        )
    ]
    for cp in loads:
        cp.start()
    pl.semaphore_wait(barrier, len(peers))

    def chunk(zz, yl, h=0, n=NH):
        at = (zz * 2 + yl) * 256 + h * PIECE
        return w.at[pl.ds(pl.multiple_of(at, PIECE), n * PIECE)]

    for i in range(HALF):
        src = w_hbm.at[i * PIECE : i * PIECE + PIECE]
        for k in (1, -1):
            go(src, chunk(z, ylo, c * HALF + i, 1), 0, wz_sem.at[z, c * HALF + i], zdev(k))
    own_half = chunk(z, ylo, c * HALF, HALF)
    go(w_hbm, own_half, 0, wy_sem.at[z], ydev(1 + 2 * c))
    go(w_hbm, own_half, 0, wp_sem.at[z], partner)

    loads[0].wait()

    def turn(i, carry):
        at = pl.multiple_of((i % 32) * 128, 128)
        gt[pl.ds(at, 128), :] = wide[0:ROWS, pl.ds(at, 128)].astype(F32).T.astype(BF16)
        return carry

    lax.fori_loop(8 * x, 8 * x + 8, turn, 0)
    gt6 = gt.reshape(NZ, 2, 2, 2, 64, 128)

    def lanes(at, n=128):
        return pl.ds(pl.multiple_of(at, 128), n)

    mine = pl.ds(2 * x, 2)
    for k in (2, 1, 3):
        to = (y + k) % 4
        go(
            gt6.at[mine, to % 2, :, to // 2],
            amat.at[mine, :, :, lanes(((4 - k) * 2 + c) * 128)],
            1,
            a_sem.at[0],
            ydev(k),
        )

    loads[1].wait()
    wide[pl.ds(ROWS, 16)] = jnp.concatenate([center_ref[...].astype(F32), jnp.zeros((12, D), F32)], 0).astype(BF16)
    acc[...] = jnp.zeros_like(acc)
    for cp in loads[2:]:
        cp.wait()

    def multiply(zz):
        at = pl.ds(pl.multiple_of(zz * 512, 512), 512)
        res = jnp.dot(wide[:, at], w[at, :], preferred_element_type=F32)
        acc[...] += res[:ROWS]
        cslot[zz] = res[ROWS : ROWS + 8]

    held = (call, sall)

    def part(b, r, cc, n=128):
        return held[b].at[pl.ds(pl.multiple_of((r * 2 + cc) * 128, 128), n)]

    def gather_own(b):
        ref = part(b, 0, c)
        go(ref, part(b, 3, c), 2, near_sem.at[b, c], ydev(1))
        go(ref, part(b, 1, c), 2, near_sem.at[b, 2 + c], ydev(3))
        go(ref, ref, 2, pair_sem.at[b], partner)

    def gather_forward(b):
        for r, cc, to in ((3, 0, 1), (1, 1, 3)):
            await_bytes(part(b, r, cc), near_sem.at[b, cc if r == 3 else 2 + cc])
            go(part(b, r, cc), part(b, 2, cc), 2, far_sem.at[b], ydev(to))

    def sums():
        gen_pre = acc[...]
        cot = part(0, 0, c)[...].astype(F32)
        part_radius = jnp.sum(jnp.abs(gen_pre).reshape(4, 32, COLS), axis=1)
        part_inner = jnp.sum((cot * gen_pre).reshape(4, 32, COLS), axis=1)
        sa[quad] = jnp.concatenate([part_radius, part_inner], 0)

    def signs():
        gen_pre = acc[...]
        sall[pl.ds(pl.multiple_of(c * 128, 128), 128)] = jnp.where(
            gen_pre > 0, 1.0, jnp.where(gen_pre < 0, -1.0, 0.0)
        ).astype(BF16)
        gather_own(1)
        gather_own(0)

    def relax():
        center_pre = cslot[0][0:4]
        for i in range(1, NZ):
            center_pre = center_pre + cslot[i][0:4]
        center_pre = center_pre + bias_ref[...]
        total = tot[...]
        phase = phase_ref[...]
        (slope, center_out, offset), pull = jax.vjp(lambda a, b: neuron(a, b, phase), center_pre, total[0:4])
        g_center, g_radius = pull((total[4:8], ccot_ref[...], ocot_ref[...]))
        return slope, center_out, offset, g_center, g_radius

    def outputs(slope, center_out, offset):
        cout_ref[...] = center_out
        off_ref[...] = offset
        gout_ref[...] = (slope[:, None, :] * acc[...].reshape(4, 32, COLS)).astype(BF16).reshape(ROWS, COLS)

    def centers(g_center):
        center_back = g_center.astype(BF16).astype(F32)
        bias_part = jnp.sum(g_center, axis=0, keepdims=True)
        xb[yhi, :, 0:COLS] = jnp.concatenate([center_back, bias_part, jnp.zeros((3, COLS), F32)], 0)
        chunk_of = jnp.concatenate([center_ref[:, lanes(me * 128)].astype(F32), jnp.zeros((4, 128), F32)], 0)
        xb[yhi, :, COLS:] = jnp.concatenate([chunk_of, jnp.zeros((8, COLS - 128), F32)], 1)
        go(xb.at[yhi], xb.at[yhi], 2, gx_sem.at[1], ydev(2, c))
        return center_back

    other = 1 - yhi

    def center_term():
        await_bytes(xb.at[other], gx_sem.at[1])
        xall = xb[:, :, 0 : COLS + 128].reshape(16, COLS + 128)
        bg_ref[...] = xall[4:5, :COLS] + xall[12:13, :COLS]
        return lax.dot_general(
            xall[:, COLS:].T.astype(BF16), xall[:, :COLS].astype(BF16), (((1,), (0,)), ((), ())), preferred_element_type=F32
        )

    def weight_out(term, count):
        for q in range(NQ):
            await_bytes(fx.at[0:count, q], f_sem.at[q])
            at = q * FQ
            wg_ref[:, at : at + FQ] = fx[:, q].astype(F32).reshape(128, FQ) + term[:, at : at + FQ]

    def drain(role):
        for group, count in enumerate(sent[role]):
            if count:
                ref = w.at[pl.ds(0, count // (COLS * 2))]
                copy_to(ref, ref, group, out_sem.at[group], partner).wait_send()

    @pl.when(c == 0)
    def _():
        roles[:] = [0]
        lax.fori_loop(8 * x + 8, 8 * x + 32, turn, 0)
        go(gt6.at[:, ylo, :, yhi], amat.at[:, :, :, lanes(0)], 1, a_sem.at[2], partner)
        for d in range(5):
            for dz in zsteps(d):
                zz = (z + NZ + dz) % NZ
                await_bytes(w.at[pl.ds(0, 384 if d == 0 else 512)], wp_sem.at[zz])
                multiply(zz)
        sums()
        for to in (partner, dev(z, yhi * 2 + 1 - ylo, 1)):
            go(sa.at[quad], sa.at[quad], 1, s_sem.at[0], to)
        signs()
        await_bytes(tot, s_sem.at[2])
        slope, center_out, offset, g_center, g_radius = relax()
        for b in (0, 1):
            await_bytes(part(b, 0, 1), pair_sem.at[b])
        for cc, at in ((0, 0), (1, 144)):
            cot = part(0, 0, cc)[...].astype(F32).reshape(4, 32, COLS)
            sign = part(1, 0, cc)[...].astype(F32).reshape(4, 32, COLS)
            back = slope[:, None, :] * cot + sign * g_radius[:, None, :]
            bk[at : at + ROWS] = back.astype(BF16).reshape(ROWS, COLS)
        bk[ROWS:144] = jnp.concatenate([centers(g_center), jnp.zeros((12, COLS), F32)], 0).astype(BF16)

        def partial(k):
            at = pl.ds(pl.multiple_of(((x + k) % 4) * 1024, 1024), 1024)
            return lax.dot_general(bk[...], w[at, :], (((1,), (1,)), ((), ())), preferred_element_type=F32)

        first, second = pl.ds(0, 144), pl.ds(144, 128)
        right, left = xdev(1, 0), xdev(3, 0)
        gs[0] = partial(2).astype(BF16)
        go(gs.at[0, first], gi.at[0, first], 2, gx_sem.at[0], right)
        go(gs.at[0, second], gi.at[0, second], 2, gx_sem.at[4], left)
        gown[...] = partial(1)
        gs[1, second] = gown[second].astype(BF16)
        go(gs.at[1, second], gr.at[0, pl.ds(0, 128)], 2, gx_sem.at[5], xdev(1, 1))
        keep[first] = gown[first]
        gown[...] = partial(3)
        gs[2, first] = gown[first].astype(BF16)
        go(gs.at[2, first], gr.at[1], 2, gx_sem.at[5], left)
        keep[second] = gown[second]
        gown[...] = partial(0)
        go(gown.at[second], gown.at[second], 2, gx_sem.at[3], partner)
        await_bytes(gi.at[0, first], gx_sem.at[0])
        gs[1, first] = (keep[first] + gi[0, first].astype(F32)).astype(BF16)
        go(gs.at[1, first], gr.at[0], 2, gx_sem.at[5], right)
        await_bytes(gi.at[0, second], gx_sem.at[4])
        gs[2, second] = (keep[second] + gi[0, second].astype(F32)).astype(BF16)
        go(gs.at[2, second], gr.at[1, pl.ds(0, 128)], 2, gx_sem.at[5], xdev(3, 1))
        outputs(slope, center_out, offset)
        term = center_term()
        await_bytes(gr, gx_sem.at[5])
        summed = gown[first] + gr[0].astype(F32) + gr[1].astype(F32)
        gg_ref[...] = summed[:ROWS]
        cg_ref[...] = summed[ROWS : ROWS + 4]
        gc[...] = summed[ROWS:]
        go(gc, gc, 2, gx_sem.at[0], partner)
        weight_out(term, 2)
        drain(0)

    @pl.when(c == 1)
    def _():
        roles[:] = [1]

        def to_partner(zz, yl):
            go(chunk(zz, yl), chunk(zz, yl), 3, wp_sem.at[zz], partner)

        def handle_y(d):
            for dz in zsteps(d):
                zz = (z + NZ + dz) % NZ
                await_bytes(chunk(zz, 1 - ylo), wy_sem.at[zz])
                to_partner(zz, 1 - ylo)

        def compute(d):
            for dz in zsteps(d):
                multiply((z + NZ + dz) % NZ)

        for d in (1, 2, 3, 4):
            for i in range(NH):
                for way in (0, 1):
                    h = (i + HALF) % NH if way == 0 else i
                    far = (h >= HALF) == (way == 0)
                    if d == 4 and not far:
                        continue
                    zz = (z + NZ - d) % NZ if way == 0 else (z + d) % NZ
                    ref = chunk(zz, ylo, h, 1)
                    await_bytes(ref, wz_sem.at[zz, h])
                    if d < 3 or (d == 3 and far):
                        go(ref, ref, 0, wz_sem.at[zz, h], zdev(1 if way == 0 else -1))
                    to = ydev(1 if h < HALF else 3)
                    if d >= 3:
                        go(ref, ref, 0, wy_sem.at[zz], to)
                    elif i % HALF == HALF - 1:
                        ref = chunk(zz, ylo, 0 if h < HALF else HALF, HALF)
                        go(ref, ref, 0, wy_sem.at[zz], to)
            for dz in zsteps(d):
                to_partner((z + NZ + dz) % NZ, ylo)
            if d >= 2:
                handle_y(d - 2)
            if d == 2:
                await_bytes(chunk(z, ylo, 0, HALF), wp_sem.at[z])
                ref = amat.at[mine, :, :, lanes(256, 768)]
                await_bytes(ref, a_sem.at[0])
                for k in (2, 1, 3):
                    go(ref, ref, 1, a_sem.at[1], xdev(k, 1))
            if d >= 2:
                compute(d - 2)
        handle_y(3)
        compute(3)
        handle_y(4)
        compute(4)

        sums()
        go(sa.at[quad], sa.at[quad], 1, s_sem.at[0], dev(z, yhi * 2 + 1 - ylo, 1))
        signs()
        lax.fori_loop(8 * x + 8, 8 * x + 20, turn, 0)
        await_bytes(sa.at[pl.ds(0, 3)], s_sem.at[0])
        sb[z] = (sa[0] + sa[1]) + (sa[2] + sa[3])
        for k in (4, 3, 5, 2, 6, 1, 7):
            go(sb.at[z], sb.at[z], 1, s_sem.at[1], zdev(k))
        lax.fori_loop(8 * x + 20, 8 * x + 32, turn, 0)
        own_a = pltpu.make_async_copy(gt6.at[:, ylo, :, yhi], amat.at[:, :, :, lanes(128)], load_sem.at[8])
        own_a.start()
        gather_forward(1)
        await_bytes(sb.at[pl.ds(0, NZ - 1)], s_sem.at[1])
        tot[...] = ((sb[0] + sb[1]) + (sb[2] + sb[3])) + ((sb[4] + sb[5]) + (sb[6] + sb[7]))
        go(tot, tot, 1, s_sem.at[2], partner)
        slope, center_out, offset, g_center, g_radius = relax()
        xs[yhi] = jnp.concatenate([slope, g_radius], 0)
        go(xs.at[yhi], xs.at[yhi], 2, gx_sem.at[2], ydev(3 - 2 * ylo))
        gather_forward(0)
        centers(g_center)

        def c_pass(r, box, at, n, first=False):
            cols = pl.ds(at, n)
            rows = pl.ds(pl.multiple_of(r * 256, 256), 256)
            scale = xs[box, 0:4, cols][None, :, None, :]
            g_rad = xs[box, 4:8, cols][None, :, None, :]
            cots = call[rows, cols].astype(F32).reshape(2, 4, 32, n)
            marks = sall[rows, cols].astype(F32).reshape(2, 4, 32, n)
            back = (scale * cots + marks * g_rad).astype(BF16).reshape(256, n)
            a = amat[:, :, :, lanes(r * 256, 256)].reshape(1024, 256)
            res = jnp.dot(a, back, preferred_element_type=F32).reshape(NZ, 128, n)
            if first:
                cmat[:, :, cols] = res
            else:
                cmat[:, :, cols] += res

        def z_step(dist, q):
            for way in (0, 1):
                longest = 4 if q % 2 == way else 3
                if dist > longest:
                    continue
                val = cmat[(z + NZ + (dist if way == 0 else -dist)) % NZ, :, pl.ds(q * FQ, FQ)]
                if dist < longest:
                    await_bytes(zr.at[way, dist, q], wz_sem.at[way * 4 + dist, q])
                    val = val + zr[way, dist, q].astype(F32)
                if dist > 0:
                    zs[way, dist, q] = val.astype(BF16)
                    to = zdev(1 if way == 0 else -1)
                    go(zs.at[way, dist, q], zr.at[way, dist - 1, q], 2, wz_sem.at[way * 4 + dist - 1, q], to)
                elif way == 1:
                    val = val + zr[0, 0, q].astype(F32)
                    fs[q] = val.astype(BF16)
                    fx[yhi, q] = val[64:].astype(BF16)
                    go(fs.at[q, 64:128], fx.at[yhi, q], 2, f_sem.at[q], ydev(2, 1))
                    go(fs.at[q, 0:64], fx.at[yhi, q], 2, f_sem.at[q], ydev(2, 0))
                    go(fs.at[q, 0:64], fx.at[yhi, q], 2, f_sem.at[q], partner)

        own_a.wait()
        await_bytes(amat.at[:, :, :, lanes(0)], a_sem.at[2])
        for b in (0, 1):
            await_bytes(part(b, 0, 0), pair_sem.at[b])
        c_pass(0, yhi, 0, COLS, first=True)
        await_bytes(w.at[pl.ds(0, 1152)], a_sem.at[1])
        for b in (0, 1):
            await_bytes(part(b, 3, 1), near_sem.at[b, 1])
            await_bytes(part(b, 1, 0), near_sem.at[b, 2])
        c_pass(1 + 2 * ylo, yhi, 0, COLS)
        await_bytes(xs.at[other], gx_sem.at[2])
        c_pass(3 - 2 * ylo, other, 0, COLS)
        for b in (0, 1):
            await_bytes(part(b, 2, 0, 256), far_sem.at[b])
        for p in (0, 1):
            c_pass(2, other, p * 256, 256)
            for q in range(p * NQ // 2, (p + 1) * NQ // 2):
                z_step(4, q)
        outputs(slope, center_out, offset)
        for dist in (3, 2, 1, 0):
            if dist == 0:
                term = center_term()
            for q in range(NQ):
                z_step(dist, q)
        second = pl.ds(144, 128)
        await_bytes(gr.at[:, pl.ds(0, 128)], gx_sem.at[5])
        await_bytes(gown.at[second], gx_sem.at[3])
        gg_ref[...] = gown[second] + gr[0, 0:128].astype(F32) + gr[1, 0:128].astype(F32)
        await_bytes(gc, gx_sem.at[0])
        cg_ref[...] = gc[0:4]
        weight_out(term, 1)
        drain(1)


def finish(*refs):
    for src, dst in zip(refs[:7], refs[7:]):
        dst[...] = src[...]


def body(gens, center, weight, bias, phase, gens_cot, center_cot, offset_cot):
    vm = pl.BlockSpec(memory_space=pltpu.VMEM)
    hbm = pl.BlockSpec(memory_space=pltpu.HBM)
    dma = pltpu.SemaphoreType.DMA
    sds = jax.ShapeDtypeStruct
    outs = pl.pallas_call(
        kernel,
        out_shape=(
            sds((4, COLS), F32),
            sds((ROWS, COLS), BF16),
            sds((4, COLS), F32),
            sds((128, COLS), F32),
            sds((1, COLS), F32),
            sds((ROWS, 1024), F32),
            sds((4, 1024), F32),
        ),
        in_specs=[hbm] * 8,
        out_specs=(vm,) * 7,
        scratch_shapes=[
            pltpu.VMEM((4, D), BF16),
            pltpu.VMEM((1, COLS), F32),
            pltpu.VMEM((4, COLS), jnp.int32),
            pltpu.VMEM((4, COLS), F32),
            pltpu.VMEM((4, COLS), F32),
            pltpu.VMEM((D, COLS), BF16),
            pltpu.VMEM((WIDE, D), BF16),
            pltpu.VMEM((ROWS, COLS), F32),
            pltpu.VMEM((NZ, 8, COLS), F32),
            pltpu.VMEM((D, ROWS), BF16),
            pltpu.VMEM((NZ, 2, 64, 1024), BF16),
            pltpu.VMEM((4, 8, COLS), F32),
            pltpu.VMEM((NZ, 8, COLS), F32),
            pltpu.VMEM((8, COLS), F32),
            pltpu.VMEM((272, COLS), BF16),
            pltpu.VMEM((1024, COLS), BF16),
            pltpu.VMEM((1024, COLS), BF16),
            pltpu.VMEM((2, 8, COLS), F32),
            pltpu.VMEM((NZ, 128, COLS), F32),
            pltpu.VMEM((2, 5, NQ, 128, FQ), BF16),
            pltpu.VMEM((2, 5, NQ, 128, FQ), BF16),
            pltpu.VMEM((3, 272, 1024), BF16),
            pltpu.VMEM((1, 272, 1024), BF16),
            pltpu.VMEM((2, 144, 1024), BF16),
            pltpu.VMEM((272, 1024), F32),
            pltpu.VMEM((272, 1024), F32),
            pltpu.VMEM((16, 1024), F32),
            pltpu.VMEM((NQ, 128, FQ), BF16),
            pltpu.VMEM((2, NQ, 64, FQ), BF16),
            pltpu.VMEM((2, 8, 2 * COLS), F32),
            dma((9,)),
            dma((4,)),
            dma((NZ, NH)),
            dma((NZ,)),
            dma((NZ,)),
            dma((3,)),
            dma((3,)),
            dma((2, 4)),
            dma((2,)),
            dma((2,)),
            dma((NQ,)),
            dma((6,)),
        ],
        compiler_params=pltpu.CompilerParams(
            collective_id=0, has_side_effects=True, vmem_limit_bytes=32 * 1024 * 1024
        ),
        name="zonotope_step",
    )(
        *(
            pltpu.with_memory_space_constraint(v, pltpu.HBM)
            for v in (
                gens.reshape(ROWS, D), center, weight, bias.reshape(1, COLS), phase,
                gens_cot.reshape(ROWS, COLS), center_cot, offset_cot,
            )
        )
    )
    outs = pl.pallas_call(
        finish,
        out_shape=tuple(sds(o.shape, o.dtype) for o in outs),
        in_specs=[vm] * 7,
        out_specs=(vm,) * 7,
        compiler_params=pltpu.CompilerParams(vmem_limit_bytes=8 * 1024 * 1024),
        name="finish",
    )(*outs)
    center_out, gens_out, offset, weight_grad, bias_grad, gens_grad, center_grad = outs
    return (
        center_out, gens_out.reshape(4, 32, COLS), offset, weight_grad, bias_grad.reshape(COLS),
        gens_grad.reshape(4, 32, 1024), center_grad,
    )


def solution(mesh):
    return jax.shard_map(
        body,
        mesh=mesh,
        in_specs=(
            P("box", "gen", None),
            P("box", None),
            P("gen", "neur"),
            P("neur"),
            P("box", "neur"),
            P("box", "gen", "neur"),
            P("box", "neur"),
            P("box", "neur"),
        ),
        out_specs=(
            P("box", "neur"),
            P("box", "gen", "neur"),
            P("box", "neur"),
            P("gen", "neur"),
            P("neur"),
            P("box", "gen", "neur"),
            P("box", "neur"),
        ),
        check_vma=False,
    )
```

time: 407 us -> 56.7 us (0.14)
  waiting for transfers between devices: 266 us -> 0 us
  blocking collectives: 108 us -> 0 us
  Pallas kernels: 0 us -> 55.9 us
  between operations: 13.9 us -> 0.64 us
  matrix products: 13 us -> 0 us
  local copies, waits for them, and re-layouts: 4.95 us -> 0 us
    reduce_scatter x2 -> x0, waiting for transfers between devices: 157 us -> none  [the longest x1 127 us: body(): lax.psum_scatter(lax.dot_general(wide, back_owned, (((0,), (0,)), ((), ()...]
    psum x2 -> x0, blocking collectives: 108 us -> none  [the longest x1 102 us: body(): radius = lax.psum(part_radius, 'gen')]
    all_gather x1 -> x0, waiting for transfers between devices: 72.6 us -> none  [body(): full_weight = lax.all_gather(weight, 'gen', axis=0, tiled=True)]
    pallas_call x0 -> x2, Pallas kernels: none -> 55.9 us  [the longest x1 54.9 us: body(): pl.pallas_call(kernel, out_shape=(sds((4, COLS), F32), sds((ROWS, COLS),...]
    psum x1 -> x0, waiting for transfers between devices: 35.1 us -> none  [body(): weight_grad, bias_grad = lax.psum((shares, bias_part), 'box')]
    dot_general x3 -> x0, matrix products: 13 us -> none  [the longest x1 5.06 us: body(): lax.dot_general(back, full_weight, (((1,), (1,)), ((), ())), preferred_el...]
  transfers between devices with their start and end apart: 4 -> 0, of which waited for: 4 -> 0; matrix products, arithmetic and copies ran while one was open for 2% -> 0% of each run, Pallas kernels for 0% -> 0%
where the time goes in v4:
time: 56.7 us; the launch traced here: 56.6 us
  Pallas kernels  55.9 us (99%)
  between operations  0.64 us (1%)
    pallas_call x1, Pallas kernels, body(): pl.pallas_call(kernel, out_shape=(sds((4, COLS), F32), sds((ROWS, COLS),...  54.9 us

profile of v4, /device:TPU:1, one launch (start us, length us, event | category | flops | bytes accessed | tf_op | source)
XLA Modules:
  0.0 56.6 jit_solution(486045943514132422)
XLA Ops:
  0.6 54.9 %zonotope_step.1 = (f32[4,512]{1,0:T(4,128)S(1)}, bf16[128,512]{1,0:T(8,128)(2,1)S(1)}, f32[4,512]{1,0:T(4,128)S(1)}, f32[128,512]{1,0:T(8,128)S(1)}, f32[1,512]...) custom-call(bf16[128,4096]{1,0:T(8,128)(2,1)} %bitcast.6, bf16[4,4096]{1,0:T(4,128)(2,1)} %center_hbm.1, ...), custom_call_target="tpu_custom_call" | custom-call | tf_op jit(solution)/shard_map/zonotope_step/pallas_call | solution.py:457
  55.6 1.0 %finish.1 = (f32[4,512]{1,0:T(4,128)}, bf16[128,512]{1,0:T(8,128)(2,1)}, f32[4,512]{1,0:T(4,128)}, f32[128,512]{1,0:T(8,128)}, f32[1,512]{1,0:T(1,128)}, /*index=5*/f32[128,1024]{1,0:T(8,128)}, f32[4,1024]{1,0:T(4,128)}) custom-call(f32[4,512]{1,0:T(4,128)S(1)} %get-tuple-element.21.refs_0_, bf16[128,512]{1,0:T(8,128)(2,1)S(1)} %get-tuple-element.22.refs_1_, ...), custom_call_target="tpu_custom_call" | custom-call | tf_op jit(solution)/shard_map/finish/pallas_call | solution.py:527

commit v5 on v4

--- a/solution.py
+++ b/solution.py
@@ -15,7 +15,6 @@
 D = 4096
 COLS = 512
 ROWS = 128
-WIDE = 144
 NH = 4
 PIECE = 256 // NH
 HALF = NH // 2
@@ -52,7 +51,6 @@
     ylo = (me // 2) % 2
     c = me % 2
     y = yhi * 2 + ylo
-    quad = ylo * 2 + c
 
     def dev(zz, yy, cc, xx=None):
         return (zz * 4 + (yy % 2) * 2 + cc, x if xx is None else xx, yy // 2)
@@ -99,7 +97,7 @@
         pltpu.make_async_copy(src, dst, load_sem.at[i])
         for i, (src, dst) in enumerate(
             (
-                (gens_hbm, wide.at[pl.ds(0, ROWS)]),
+                (gens_hbm, wide.at[pl.ds(pl.multiple_of(c * 144, 16), ROWS)]),
                 (center_hbm, center_ref),
                 (w_hbm, w.at[pl.ds(pl.multiple_of(me * 128, 128), 128)]),
                 (bias_hbm, bias_ref),
@@ -126,11 +124,19 @@
     go(w_hbm, own_half, 0, wy_sem.at[z], ydev(1 + 2 * c))
     go(w_hbm, own_half, 0, wp_sem.at[z], partner)
 
+    @pl.when(c == 0)
+    def _():
+        roles[:] = [0]
+        go(gens_hbm, wide.at[pl.ds(0, ROWS)], 3, a_sem.at[3], partner)
+        go(cot_hbm, call.at[pl.ds(0, ROWS)], 2, pair_sem.at[0], partner)
+
+    roles[:] = [0, 1]
+
     loads[0].wait()
 
     def turn(i, carry):
         at = pl.multiple_of((i % 32) * 128, 128)
-        gt[pl.ds(at, 128), :] = wide[0:ROWS, pl.ds(at, 128)].astype(F32).T.astype(BF16)
+        gt[pl.ds(at, 128), :] = wide[pl.ds(pl.multiple_of(c * 144, 16), ROWS), pl.ds(at, 128)].astype(F32).T.astype(BF16)
         return carry
 
     lax.fori_loop(8 * x, 8 * x + 8, turn, 0)
@@ -156,10 +162,12 @@
     for cp in loads[2:]:
         cp.wait()
 
-    def multiply(zz):
+    def multiply(zz, rows):
         at = pl.ds(pl.multiple_of(zz * 512, 512), 512)
-        res = jnp.dot(wide[:, at], w[at, :], preferred_element_type=F32)
-        acc[...] += res[:ROWS]
+        res = jnp.dot(wide[0:rows, at], w[at, :], preferred_element_type=F32)
+        acc[0:ROWS] += res[:ROWS]
+        if rows > 144:
+            acc[ROWS:] += res[144:]
         cslot[zz] = res[ROWS : ROWS + 8]
 
     held = (call, sall)
@@ -168,30 +176,20 @@
         return held[b].at[pl.ds(pl.multiple_of((r * 2 + cc) * 128, 128), n)]
 
     def gather_own(b):
-        ref = part(b, 0, c)
-        go(ref, part(b, 3, c), 2, near_sem.at[b, c], ydev(1))
-        go(ref, part(b, 1, c), 2, near_sem.at[b, 2 + c], ydev(3))
-        go(ref, ref, 2, pair_sem.at[b], partner)
+        for cc in (0, 1):
+            ref = part(b, 0, cc)
+            go(ref, part(b, 3, cc), 2, near_sem.at[b, cc], ydev(1))
+            go(ref, part(b, 1, cc), 2, near_sem.at[b, 2 + cc], ydev(3))
+        go(part(b, 0, 1), part(b, 0, 1), 2, pair_sem.at[b], partner)
 
     def gather_forward(b):
         for r, cc, to in ((3, 0, 1), (1, 1, 3)):
             await_bytes(part(b, r, cc), near_sem.at[b, cc if r == 3 else 2 + cc])
             go(part(b, r, cc), part(b, 2, cc), 2, far_sem.at[b], ydev(to))
 
-    def sums():
-        gen_pre = acc[...]
-        cot = part(0, 0, c)[...].astype(F32)
-        part_radius = jnp.sum(jnp.abs(gen_pre).reshape(4, 32, COLS), axis=1)
-        part_inner = jnp.sum((cot * gen_pre).reshape(4, 32, COLS), axis=1)
-        sa[quad] = jnp.concatenate([part_radius, part_inner], 0)
-
-    def signs():
-        gen_pre = acc[...]
-        sall[pl.ds(pl.multiple_of(c * 128, 128), 128)] = jnp.where(
-            gen_pre > 0, 1.0, jnp.where(gen_pre < 0, -1.0, 0.0)
-        ).astype(BF16)
-        gather_own(1)
-        gather_own(0)
+    def signs(n):
+        gen_pre = acc[0:n]
+        sall[0:n] = jnp.where(gen_pre > 0, 1.0, jnp.where(gen_pre < 0, -1.0, 0.0)).astype(BF16)
 
     def relax():
         center_pre = cslot[0][0:4]
@@ -207,7 +205,8 @@
     def outputs(slope, center_out, offset):
         cout_ref[...] = center_out
         off_ref[...] = offset
-        gout_ref[...] = (slope[:, None, :] * acc[...].reshape(4, 32, COLS)).astype(BF16).reshape(ROWS, COLS)
+        gen_pre = acc[pl.ds(pl.multiple_of(c * ROWS, ROWS), ROWS)].reshape(4, 32, COLS)
+        gout_ref[...] = (slope[:, None, :] * gen_pre).astype(BF16).reshape(ROWS, COLS)
 
     def centers(g_center):
         center_back = g_center.astype(BF16).astype(F32)
@@ -249,11 +248,8 @@
             for dz in zsteps(d):
                 zz = (z + NZ + dz) % NZ
                 await_bytes(w.at[pl.ds(0, 384 if d == 0 else 512)], wp_sem.at[zz])
-                multiply(zz)
-        sums()
-        for to in (partner, dev(z, yhi * 2 + 1 - ylo, 1)):
-            go(sa.at[quad], sa.at[quad], 1, s_sem.at[0], to)
-        signs()
+                multiply(zz, 144)
+        signs(ROWS)
         await_bytes(tot, s_sem.at[2])
         slope, center_out, offset, g_center, g_radius = relax()
         for b in (0, 1):
@@ -316,8 +312,10 @@
 
         def compute(d):
             for dz in zsteps(d):
-                multiply((z + NZ + dz) % NZ)
-
+                multiply((z + NZ + dz) % NZ, 272)
+
+        await_bytes(wide.at[pl.ds(0, ROWS)], a_sem.at[3])
+        await_bytes(part(0, 0, 0), pair_sem.at[0])
         for d in (1, 2, 3, 4):
             for i in range(NH):
                 for way in (0, 1):
@@ -338,6 +336,8 @@
                         go(ref, ref, 0, wy_sem.at[zz], to)
             for dz in zsteps(d):
                 to_partner((z + NZ + dz) % NZ, ylo)
+            if d == 4:
+                gather_own(0)
             if d >= 2:
                 handle_y(d - 2)
             if d == 2:
@@ -353,25 +353,30 @@
         handle_y(4)
         compute(4)
 
-        sums()
-        go(sa.at[quad], sa.at[quad], 1, s_sem.at[0], dev(z, yhi * 2 + 1 - ylo, 1))
-        signs()
+        gen_pre = acc[...].reshape(2, 4, 32, COLS)
+        cot = call[0:256].astype(F32).reshape(2, 4, 32, COLS)
+        part_radius = jnp.sum(jnp.abs(gen_pre), axis=(0, 2))
+        part_inner = jnp.sum(cot * gen_pre, axis=(0, 2))
+        sa[ylo] = jnp.concatenate([part_radius, part_inner], 0)
+        go(sa.at[ylo], sa.at[ylo], 1, s_sem.at[0], dev(z, yhi * 2 + 1 - ylo, 1))
+        signs(256)
+        gather_own(1)
         lax.fori_loop(8 * x + 8, 8 * x + 20, turn, 0)
-        await_bytes(sa.at[pl.ds(0, 3)], s_sem.at[0])
-        sb[z] = (sa[0] + sa[1]) + (sa[2] + sa[3])
+        await_bytes(sa.at[1 - ylo], s_sem.at[0])
+        sb[z] = sa[0] + sa[1]
         for k in (4, 3, 5, 2, 6, 1, 7):
             go(sb.at[z], sb.at[z], 1, s_sem.at[1], zdev(k))
         lax.fori_loop(8 * x + 20, 8 * x + 32, turn, 0)
         own_a = pltpu.make_async_copy(gt6.at[:, ylo, :, yhi], amat.at[:, :, :, lanes(128)], load_sem.at[8])
         own_a.start()
-        gather_forward(1)
+        gather_forward(0)
         await_bytes(sb.at[pl.ds(0, NZ - 1)], s_sem.at[1])
         tot[...] = ((sb[0] + sb[1]) + (sb[2] + sb[3])) + ((sb[4] + sb[5]) + (sb[6] + sb[7]))
         go(tot, tot, 1, s_sem.at[2], partner)
         slope, center_out, offset, g_center, g_radius = relax()
         xs[yhi] = jnp.concatenate([slope, g_radius], 0)
         go(xs.at[yhi], xs.at[yhi], 2, gx_sem.at[2], ydev(3 - 2 * ylo))
-        gather_forward(0)
+        gather_forward(1)
         centers(g_center)
 
         def c_pass(r, box, at, n, first=False):
@@ -391,19 +396,22 @@
 
         def z_step(dist, q):
             for way in (0, 1):
-                longest = 4 if q % 2 == way else 3
-                if dist > longest:
+                long = q % 2 == way
+                if dist == 4 and not long:
                     continue
                 val = cmat[(z + NZ + (dist if way == 0 else -dist)) % NZ, :, pl.ds(q * FQ, FQ)]
-                if dist < longest:
-                    await_bytes(zr.at[way, dist, q], wz_sem.at[way * 4 + dist, q])
-                    val = val + zr[way, dist, q].astype(F32)
+                for source in {2: (3, 4) if long else (3,), 1: (2,), 0: (1,)}.get(dist, ()):
+                    await_bytes(zr.at[way, source, q], wz_sem.at[way * 4 + source - 1, q])
+                    val = val + zr[way, source, q].astype(F32)
                 if dist > 0:
                     zs[way, dist, q] = val.astype(BF16)
-                    to = zdev(1 if way == 0 else -1)
-                    go(zs.at[way, dist, q], zr.at[way, dist - 1, q], 2, wz_sem.at[way * 4 + dist - 1, q], to)
-                elif way == 1:
-                    val = val + zr[0, 0, q].astype(F32)
+                    hops = 2 if dist == 4 else 1
+                    to = zdev(hops if way == 0 else -hops)
+                    go(zs.at[way, dist, q], zr.at[way, dist, q], 2, wz_sem.at[way * 4 + dist - 1, q], to)
+                elif way == 0:
+                    first = zr[0, 1, q].astype(F32)
+                else:
+                    val = first + val
                     fs[q] = val.astype(BF16)
                     fx[yhi, q] = val[64:].astype(BF16)
                     go(fs.at[q, 64:128], fx.at[yhi, q], 2, f_sem.at[q], ydev(2, 1))
@@ -412,8 +420,6 @@
 
         own_a.wait()
         await_bytes(amat.at[:, :, :, lanes(0)], a_sem.at[2])
-        for b in (0, 1):
-            await_bytes(part(b, 0, 0), pair_sem.at[b])
         c_pass(0, yhi, 0, COLS, first=True)
         await_bytes(w.at[pl.ds(0, 1152)], a_sem.at[1])
         for b in (0, 1):
@@ -428,8 +434,9 @@
             c_pass(2, other, p * 256, 256)
             for q in range(p * NQ // 2, (p + 1) * NQ // 2):
                 z_step(4, q)
+                z_step(3, q)
         outputs(slope, center_out, offset)
-        for dist in (3, 2, 1, 0):
+        for dist in (2, 1, 0):
             if dist == 0:
                 term = center_term()
             for q in range(NQ):
@@ -474,12 +481,12 @@
             pltpu.VMEM((4, COLS), F32),
             pltpu.VMEM((4, COLS), F32),
             pltpu.VMEM((D, COLS), BF16),
-            pltpu.VMEM((WIDE, D), BF16),
-            pltpu.VMEM((ROWS, COLS), F32),
+            pltpu.VMEM((272, D), BF16),
+            pltpu.VMEM((2 * ROWS, COLS), F32),
             pltpu.VMEM((NZ, 8, COLS), F32),
             pltpu.VMEM((D, ROWS), BF16),
             pltpu.VMEM((NZ, 2, 64, 1024), BF16),
-            pltpu.VMEM((4, 8, COLS), F32),
+            pltpu.VMEM((2, 8, COLS), F32),
             pltpu.VMEM((NZ, 8, COLS), F32),
             pltpu.VMEM((8, COLS), F32),
             pltpu.VMEM((272, COLS), BF16),
@@ -503,7 +510,7 @@
             dma((NZ, NH)),
             dma((NZ,)),
             dma((NZ,)),
-            dma((3,)),
+            dma((4,)),
             dma((3,)),
             dma((2, 4)),
             dma((2,)),

time: 56.7 us -> 54.1 us (0.954)
  Pallas kernels: 55.9 us -> 53.4 us
    pallas_call x1, Pallas kernels: 54.9 us -> 52.4 us  [body(): pl.pallas_call(kernel, out_shape=(sds((4, COLS), F32), sds((ROWS, COLS),...]
where the time goes in v5:
time: 54.1 us; the launch traced here: 54 us
  Pallas kernels  53.4 us (99%)
  between operations  0.64 us (1%)
    pallas_call x1, Pallas kernels, body(): pl.pallas_call(kernel, out_shape=(sds((4, COLS), F32), sds((ROWS, COLS),...  52.4 us

profile of v5, /device:TPU:1, one launch (start us, length us, event | category | flops | bytes accessed | tf_op | source)
XLA Modules:
  0.0 54.0 jit_solution(5412542429522733963)
XLA Ops:
  0.6 52.4 %zonotope_step.1 = (f32[4,512]{1,0:T(4,128)S(1)}, bf16[128,512]{1,0:T(8,128)(2,1)S(1)}, f32[4,512]{1,0:T(4,128)S(1)}, f32[128,512]{1,0:T(8,128)S(1)}, f32[1,512]...) custom-call(bf16[128,4096]{1,0:T(8,128)(2,1)} %bitcast.6, bf16[4,4096]{1,0:T(4,128)(2,1)} %center_hbm.1, ...), custom_call_target="tpu_custom_call" | custom-call | tf_op jit(solution)/shard_map/zonotope_step/pallas_call | solution.py:464
  53.0 1.0 %finish.1 = (f32[4,512]{1,0:T(4,128)}, bf16[128,512]{1,0:T(8,128)(2,1)}, f32[4,512]{1,0:T(4,128)}, f32[128,512]{1,0:T(8,128)}, f32[1,512]{1,0:T(1,128)}, /*index=5*/f32[128,1024]{1,0:T(8,128)}, f32[4,1024]{1,0:T(4,128)}) custom-call(f32[4,512]{1,0:T(4,128)S(1)} %get-tuple-element.21.refs_0_, bf16[128,512]{1,0:T(8,128)(2,1)S(1)} %get-tuple-element.22.refs_1_, ...), custom_call_target="tpu_custom_call" | custom-call | tf_op jit(solution)/shard_map/finish/pallas_call | solution.py:534

commit v6 on v5

--- a/solution.py
+++ b/solution.py
@@ -177,9 +177,8 @@
 
     def gather_own(b):
         for cc in (0, 1):
-            ref = part(b, 0, cc)
-            go(ref, part(b, 3, cc), 2, near_sem.at[b, cc], ydev(1))
-            go(ref, part(b, 1, cc), 2, near_sem.at[b, 2 + cc], ydev(3))
+            go(part(b, 0, cc), part(b, 3, cc), 2, near_sem.at[b, cc], ydev(1))
+            go(part(b, 0, 1 - cc), part(b, 1, 1 - cc), 2, near_sem.at[b, 3 - cc], ydev(3))
         go(part(b, 0, 1), part(b, 0, 1), 2, pair_sem.at[b], partner)
 
     def gather_forward(b):
@@ -314,8 +313,6 @@
             for dz in zsteps(d):
                 multiply((z + NZ + dz) % NZ, 272)
 
-        await_bytes(wide.at[pl.ds(0, ROWS)], a_sem.at[3])
-        await_bytes(part(0, 0, 0), pair_sem.at[0])
         for d in (1, 2, 3, 4):
             for i in range(NH):
                 for way in (0, 1):
@@ -346,8 +343,13 @@
                 await_bytes(ref, a_sem.at[0])
                 for k in (2, 1, 3):
                     go(ref, ref, 1, a_sem.at[1], xdev(k, 1))
-            if d >= 2:
-                compute(d - 2)
+            if d == 3:
+                await_bytes(wide.at[pl.ds(0, ROWS)], a_sem.at[3])
+                await_bytes(part(0, 0, 0), pair_sem.at[0])
+                compute(0)
+            if d == 4:
+                compute(1)
+                compute(2)
         handle_y(3)
         compute(3)
         handle_y(4)
@@ -361,22 +363,22 @@
         go(sa.at[ylo], sa.at[ylo], 1, s_sem.at[0], dev(z, yhi * 2 + 1 - ylo, 1))
         signs(256)
         gather_own(1)
-        lax.fori_loop(8 * x + 8, 8 * x + 20, turn, 0)
+        lax.fori_loop(8 * x + 8, 8 * x + 16, turn, 0)
         await_bytes(sa.at[1 - ylo], s_sem.at[0])
         sb[z] = sa[0] + sa[1]
         for k in (4, 3, 5, 2, 6, 1, 7):
             go(sb.at[z], sb.at[z], 1, s_sem.at[1], zdev(k))
-        lax.fori_loop(8 * x + 20, 8 * x + 32, turn, 0)
+        gather_forward(0)
+        lax.fori_loop(8 * x + 16, 8 * x + 32, turn, 0)
         own_a = pltpu.make_async_copy(gt6.at[:, ylo, :, yhi], amat.at[:, :, :, lanes(128)], load_sem.at[8])
         own_a.start()
-        gather_forward(0)
+        gather_forward(1)
         await_bytes(sb.at[pl.ds(0, NZ - 1)], s_sem.at[1])
         tot[...] = ((sb[0] + sb[1]) + (sb[2] + sb[3])) + ((sb[4] + sb[5]) + (sb[6] + sb[7]))
         go(tot, tot, 1, s_sem.at[2], partner)
         slope, center_out, offset, g_center, g_radius = relax()
         xs[yhi] = jnp.concatenate([slope, g_radius], 0)
         go(xs.at[yhi], xs.at[yhi], 2, gx_sem.at[2], ydev(3 - 2 * ylo))
-        gather_forward(1)
         centers(g_center)
 
         def c_pass(r, box, at, n, first=False):
@@ -427,14 +429,28 @@
             await_bytes(part(b, 1, 0), near_sem.at[b, 2])
         c_pass(1 + 2 * ylo, yhi, 0, COLS)
         await_bytes(xs.at[other], gx_sem.at[2])
-        c_pass(3 - 2 * ylo, other, 0, COLS)
         for b in (0, 1):
             await_bytes(part(b, 2, 0, 256), far_sem.at[b])
-        for p in (0, 1):
-            c_pass(2, other, p * 256, 256)
-            for q in range(p * NQ // 2, (p + 1) * NQ // 2):
-                z_step(4, q)
-                z_step(3, q)
+        start = 256 * (2 - ylo)
+        rows = pl.ds(pl.multiple_of(start, 256), 512)
+        scale = xs[other, 0:4][None, :, None, :]
+        g_rad = xs[other, 4:8][None, :, None, :]
+        cots = call[rows].astype(F32).reshape(4, 4, 32, COLS)
+        marks = sall[rows].astype(F32).reshape(4, 4, 32, COLS)
+        back = (scale * cots + marks * g_rad).astype(BF16).reshape(512, COLS)
+
+        def block_pass(offsets):
+            blocks = [(z + NZ + k) % NZ for k in offsets]
+            a = jnp.concatenate([amat[zz, :, :, lanes(start, 512)].reshape(128, 512) for zz in blocks], 0)
+            res = jnp.dot(a, back, preferred_element_type=F32)
+            for i, zz in enumerate(blocks):
+                cmat[zz] += res[i * 128 : i * 128 + 128]
+
+        block_pass((4, 3, -3))
+        for q in range(NQ):
+            z_step(4, q)
+            z_step(3, q)
+        block_pass((2, -2, 1, -1, 0))
         outputs(slope, center_out, offset)
         for dist in (2, 1, 0):
             if dist == 0:

time: 54.1 us -> 51.8 us (0.957)
  Pallas kernels: 53.4 us -> 51 us
    pallas_call x1, Pallas kernels: 52.4 us -> 50 us  [body(): pl.pallas_call(kernel, out_shape=(sds((4, COLS), F32), sds((ROWS, COLS),...]
where the time goes in v6:
time: 51.8 us; the launch traced here: 51.7 us
  Pallas kernels  51 us (98%)
  between operations  0.64 us (1%)
    pallas_call x1, Pallas kernels, body(): pl.pallas_call(kernel, out_shape=(sds((4, COLS), F32), sds((ROWS, COLS),...  50 us

profile of v6, /device:TPU:1, one launch (start us, length us, event | category | flops | bytes accessed | tf_op | source)
XLA Modules:
  0.0 51.7 jit_solution(7046592837128921860)
XLA Ops:
  0.6 50.0 %zonotope_step.1 = (f32[4,512]{1,0:T(4,128)S(1)}, bf16[128,512]{1,0:T(8,128)(2,1)S(1)}, f32[4,512]{1,0:T(4,128)S(1)}, f32[128,512]{1,0:T(8,128)S(1)}, f32[1,512]...) custom-call(bf16[128,4096]{1,0:T(8,128)(2,1)} %bitcast.6, bf16[4,4096]{1,0:T(4,128)(2,1)} %center_hbm.1, ...), custom_call_target="tpu_custom_call" | custom-call | tf_op jit(solution)/shard_map/zonotope_step/pallas_call | solution.py:480
  50.7 1.0 %finish.1 = (f32[4,512]{1,0:T(4,128)}, bf16[128,512]{1,0:T(8,128)(2,1)}, f32[4,512]{1,0:T(4,128)}, f32[128,512]{1,0:T(8,128)}, f32[1,512]{1,0:T(1,128)}, /*index=5*/f32[128,1024]{1,0:T(8,128)}, f32[4,1024]{1,0:T(4,128)}) custom-call(f32[4,512]{1,0:T(4,128)S(1)} %get-tuple-element.21.refs_0_, bf16[128,512]{1,0:T(8,128)(2,1)S(1)} %get-tuple-element.22.refs_1_, ...), custom_call_target="tpu_custom_call" | custom-call | tf_op jit(solution)/shard_map/finish/pallas_call | solution.py:550

commit v7 on v6

--- a/solution.py
+++ b/solution.py
@@ -326,11 +326,7 @@
                     if d < 3 or (d == 3 and far):
                         go(ref, ref, 0, wz_sem.at[zz, h], zdev(1 if way == 0 else -1))
                     to = ydev(1 if h < HALF else 3)
-                    if d >= 3:
-                        go(ref, ref, 0, wy_sem.at[zz], to)
-                    elif i % HALF == HALF - 1:
-                        ref = chunk(zz, ylo, 0 if h < HALF else HALF, HALF)
-                        go(ref, ref, 0, wy_sem.at[zz], to)
+                    go(ref, ref, 0, wy_sem.at[zz], to)
             for dz in zsteps(d):
                 to_partner((z + NZ + dz) % NZ, ylo)
             if d == 4:
@@ -363,13 +359,12 @@
         go(sa.at[ylo], sa.at[ylo], 1, s_sem.at[0], dev(z, yhi * 2 + 1 - ylo, 1))
         signs(256)
         gather_own(1)
-        lax.fori_loop(8 * x + 8, 8 * x + 16, turn, 0)
         await_bytes(sa.at[1 - ylo], s_sem.at[0])
         sb[z] = sa[0] + sa[1]
         for k in (4, 3, 5, 2, 6, 1, 7):
             go(sb.at[z], sb.at[z], 1, s_sem.at[1], zdev(k))
         gather_forward(0)
-        lax.fori_loop(8 * x + 16, 8 * x + 32, turn, 0)
+        lax.fori_loop(8 * x + 8, 8 * x + 32, turn, 0)
         own_a = pltpu.make_async_copy(gt6.at[:, ylo, :, yhi], amat.at[:, :, :, lanes(128)], load_sem.at[8])
         own_a.start()
         gather_forward(1)

time: 51.8 us -> 51.9 us (level)
  no operation moved by 1% of the time
where the time goes in v7:
time: 51.9 us; the launch traced here: 51.8 us
  Pallas kernels  51.1 us (98%)
  between operations  0.64 us (1%)
    pallas_call x1, Pallas kernels, body(): pl.pallas_call(kernel, out_shape=(sds((4, COLS), F32), sds((ROWS, COLS),...  50.1 us

profile of v7, /device:TPU:1, one launch (start us, length us, event | category | flops | bytes accessed | tf_op | source)
XLA Modules:
  0.0 51.8 jit_solution(5642972825265268213)
XLA Ops:
  0.6 50.1 %zonotope_step.1 = (f32[4,512]{1,0:T(4,128)S(1)}, bf16[128,512]{1,0:T(8,128)(2,1)S(1)}, f32[4,512]{1,0:T(4,128)S(1)}, f32[128,512]{1,0:T(8,128)S(1)}, f32[1,512]...) custom-call(bf16[128,4096]{1,0:T(8,128)(2,1)} %bitcast.6, bf16[4,4096]{1,0:T(4,128)(2,1)} %center_hbm.1, ...), custom_call_target="tpu_custom_call" | custom-call | tf_op jit(solution)/shard_map/zonotope_step/pallas_call | solution.py:475
  50.8 1.0 %finish.1 = (f32[4,512]{1,0:T(4,128)}, bf16[128,512]{1,0:T(8,128)(2,1)}, f32[4,512]{1,0:T(4,128)}, f32[128,512]{1,0:T(8,128)}, f32[1,512]{1,0:T(1,128)}, /*index=5*/f32[128,1024]{1,0:T(8,128)}, f32[4,1024]{1,0:T(4,128)}) custom-call(f32[4,512]{1,0:T(4,128)S(1)} %get-tuple-element.21.refs_0_, bf16[128,512]{1,0:T(8,128)(2,1)S(1)} %get-tuple-element.22.refs_1_, ...), custom_call_target="tpu_custom_call" | custom-call | tf_op jit(solution)/shard_map/finish/pallas_call | solution.py:545
